TPU v7x, 512 devices: a whole 4x8x8 slice. The times are simulated.
512 devices in a mesh: tile: 32 (over z, y_lo, core), frame: 16 (over x, y_hi).
Axes of the slice: x: 4, y: 8 (y_hi: 4, y_lo: 2; y = y_hi * 2 + y_lo), z: 8, core: 2. Of those that a mesh axis runs over, the one named last changes fastest.
Arguments:
- estimate: float32 [512, 4096], P('tile'), may hold values from -6 to 6
- frames: float32 [16, 256, 2048], P('frame', 'tile'), may hold values from -4 to 4
- shifts: int32 [16, 2], P('frame'), may hold values from -5 to 5, as said below
- blur: float32 [7], replicated, may hold values from 0.2 to 1
Outputs:
- result: float32 [512, 4096], P('tile')
Inputs may be any that keep to these rules, and one draw needn't show every extreme that they name: `shifts`: some frame has a row shift of 5 and some frame a column shift of -5.
All inputs are finite; a program needn't handle non-finite values.
Results may differ from a plain program's by a relative error of at most 0.0003.
Values sent between devices are 32-bit elements; how exact they have to be, the bound alone decides.
A program may use at most 128 MiB of HBM per device.

v0:
```python
import jax
import jax.numpy as jnp
from jax import lax
from jax.sharding import PartitionSpec as P

FACTOR = 2
RADIUS = 3
WINDOW = 2
ITERS = 2
MARGIN = 8
LR_RIM = 4
RIM = 16


def padded(block, sides, width):
    for axis, dim in sides:
        count = lax.axis_size(axis)
        forward = [(i, i + 1) for i in range(count - 1)]
        backward = [(target, source) for source, target in forward]
        low = lax.ppermute(
            lax.slice_in_dim(block, block.shape[dim] - width, None, axis=dim), axis, forward
        )
        high = lax.ppermute(lax.slice_in_dim(block, 0, width, axis=dim), axis, backward)
        block = jnp.concatenate([low, block, high], axis=dim)
    return block


def band_table(taps, offset, count_out, count_in):
    outer = lax.broadcasted_iota(jnp.int32, (count_out, count_in), 0)
    inner = lax.broadcasted_iota(jnp.int32, (count_out, count_in), 1)
    index = inner - FACTOR * outer - MARGIN - offset + RADIUS
    total = jnp.zeros((count_out, count_in), jnp.float32)
    for tap in range(2 * RADIUS + 1):
        total = total + jnp.where(index == tap, taps[tap], 0.0)
    return total


def contract(left, right, left_dim, right_dim):
    return lax.dot_general(
        left,
        right,
        (((left_dim,), (right_dim,)), ((), ())),
        precision=lax.Precision.HIGHEST,
        preferred_element_type=jnp.float32,
    )


def frame_model(block, lows, shift_list, taps, live):
    height = block.shape[0] - 2 * RIM
    inner_cols = block.shape[1] - 2 * RIM
    low_rows = lows.shape[1]
    low_cols = lows.shape[2]

    def add_frame(total, item):
        low, shift = item
        table = band_table(taps, shift[0], low_rows, height + 2 * RIM)
        rows_done = jnp.dot(
            table, block, precision=lax.Precision.HIGHEST, preferred_element_type=jnp.float32
        )
        pred = jnp.zeros((low_rows, low_cols), jnp.float32)
        for tap in range(2 * RADIUS + 1):
            start = MARGIN - RADIUS + tap + shift[1]
            piece = lax.dynamic_slice_in_dim(rows_done, start, FACTOR * low_cols, 1)
            pred = pred + taps[tap] * piece.reshape(low_rows, low_cols, FACTOR)[:, :, 0]
        misfit = jnp.where(live, jnp.tanh(pred - low), 0.0)
        padding = jnp.zeros((low_rows, low_cols, FACTOR - 1), jnp.float32)
        upward = jnp.concatenate([misfit[:, :, None], padding], axis=2).reshape(
            low_rows, FACTOR * low_cols
        )
        spread = jnp.zeros((low_rows, inner_cols), jnp.float32)
        for tap in range(2 * RADIUS + 1):
            start = FACTOR * LR_RIM + RADIUS - shift[1] - tap
            spread = spread + taps[tap] * lax.dynamic_slice_in_dim(upward, start, inner_cols, 1)
        return (total + contract(table[:, RIM : RIM + height], spread, 0, 0), None)

    data, unused = lax.scan(
        add_frame, jnp.zeros((height, inner_cols), jnp.float32), (lows, shift_list)
    )
    return data


def prior_block(block, first_row, total_rows, first_col, total_cols, col_start, cols):
    height = block.shape[0] - 2 * RIM
    band_rows = height + 2 * WINDOW
    band_cols = cols + 2 * WINDOW
    centre = lax.dynamic_slice(
        block, (RIM - WINDOW, RIM + col_start - WINDOW), (band_rows, band_cols)
    )
    row_pos = first_row - WINDOW + lax.broadcasted_iota(jnp.int32, (band_rows, band_cols), 0)
    col_pos = (
        first_col + col_start - WINDOW + lax.broadcasted_iota(jnp.int32, (band_rows, band_cols), 1)
    )
    inside = (row_pos >= 0) & (row_pos < total_rows) & (col_pos >= 0) & (col_pos < total_cols)
    total = jnp.zeros((height, cols), jnp.float32)
    for down_off in range(-WINDOW, WINDOW + 1):
        for side_off in range(-WINDOW, WINDOW + 1):
            if down_off == 0 and side_off == 0:
                continue
            near = lax.dynamic_slice(
                block,
                (RIM - WINDOW + down_off, RIM + col_start - WINDOW + side_off),
                (band_rows, band_cols),
            )
            slope = jnp.where(inside, jnp.tanh((centre - near) / 0.5), 0.0)
            here = slope[WINDOW : WINDOW + height, WINDOW : WINDOW + cols]
            behind = slope[
                WINDOW - down_off : WINDOW - down_off + height,
                WINDOW - side_off : WINDOW - side_off + cols,
            ]
            total = total + 0.7 ** (abs(down_off) + abs(side_off)) * (here - behind)
    return total


def live_mask(first_row, total_rows, first_col, total_cols, low_rows, low_cols):
    row_pos = (
        first_row // FACTOR - LR_RIM + lax.broadcasted_iota(jnp.int32, (low_rows, low_cols), 0)
    )
    col_pos = (
        first_col // FACTOR - LR_RIM + lax.broadcasted_iota(jnp.int32, (low_rows, low_cols), 1)
    )
    return (
        (row_pos >= 0)
        & (row_pos < total_rows // FACTOR)
        & (col_pos >= 0)
        & (col_pos < total_cols // FACTOR)
    )


def local(estimate, frames, shifts, blur):
    height = estimate.shape[0]
    width = estimate.shape[1]
    total_rows = height * lax.axis_size("tile")
    first_row = lax.axis_index("tile") * height
    taps = blur / jnp.sum(blur)
    low_rows = height // FACTOR + 2 * LR_RIM
    rims = padded(frames, (("tile", 1),), LR_RIM)
    lows = jnp.pad(rims, ((0, 0), (0, 0), (LR_RIM, LR_RIM)))
    live = live_mask(first_row, total_rows, 0, width, low_rows, lows.shape[2])
    image = estimate
    for step in range(ITERS):
        wide = padded(image, (("tile", 0),), RIM)
        block = jnp.pad(wide, ((0, 0), (RIM, RIM)))
        data = frame_model(block, lows, shifts, taps, live)
        summed = lax.psum(data, "frame")
        smooth = prior_block(block, first_row, total_rows, 0, width, 0, width)
        image = image - 0.1 * (summed + 0.05 * smooth)
    return image


def solution(mesh):
    placed = (P("tile", None), P("frame", "tile", None), P("frame", None), P())
    return jax.shard_map(
        local, mesh=mesh, in_specs=placed, out_specs=P("tile", None), check_vma=False
    )
```

profile of v0, /device:TPU:8, one launch (start us, length us, event | category | flops | bytes accessed | tf_op | source)
XLA Modules:
  0.0 628.5 jit_solution(15337056274558258681)
XLA Ops:
  8.5 2.4 collective-permute-start
  12.4 7.3 %collective-permute-start.3 = (f32[1,4,2048]{2,1,0:T(4,128)}, f32[1,4,2048]{2,1,0:T(4,128)}, u32[]{:S(2)}, u32[]{:S(2)}) collective-permute-start(f32[1,4,2048]{2,1,0:T(4,128)} %get-tuple-element.124), channel_id=1, source_target_pairs={{16,0},{32,16},{48,32},{64,48},{80,64},{96,80},{112,96},{128,112},... | collective-permute-start | bytes 98312 | tf_op jit(solution)/shard_map/ppermute | solution.py:23
  44.4 5.1 select_add_fusion
  50.7 2.7 fusion.138
  53.4 2.7 fusion.144
  56.1 5.6 fusion.305
  64.9 2.2 slice.595
  67.1 3.4 copy.87
  72.0 2.0 slice.594
  74.0 3.4 copy.86
  78.9 2.0 slice.593
  80.9 3.4 copy.85
  85.9 2.0 slice.592
  87.9 3.4 copy.84
  92.8 2.0 slice.591
  94.8 3.4 copy.83
  98.8 2.0 slice.590
  100.8 3.4 copy.82
  104.8 2.0 slice.589
  106.8 2.4 copy.81
  109.2 5.6 tanh_select_fusion.1
  114.8 2.1 copy.109
  116.9 2.5 concatenate.19.clone
  119.4 5.3 constant_dynamic-slice_fusion.20
  124.6 2.2 copy.94
  126.8 2.3 copy.93
  129.1 2.9 copy.92
  133.3 3.0 copy.90
  136.3 2.9 copy.89
  140.5 6.9 %fusion.261 = f32[16,4096]{1,0:T(8,128)} fusion(f32[16,4096]{1,0:T(8,128)S(1)} %copy.94, f32[16,4096]{1,0:T(8,128)S(1)} %copy.93, f32[16,4096]{1,0:T(8,128)} %copy.92, f32[16,4096]{1,0:T(8,128)} %copy.91, f32[16,4096]{1,0:T(8,128)} %copy.90, f32[16,4096]{1,0:T(8,128)} %copy.89, f32[16,4096]{1,0:T(8,128)} %copy.88, f32[]{:T(128)} %bitcast.7, f32[]{:T(128)} %bitcast.6, ...), kind=kOutput, calls=%fused_computation.364 | convolution fusion | flops 13434880 | bytes 2100252 | tf_op jit(solution)/shard_map/while/body/eval_jaxpr/dot_general | solution.py:39
  147.7 2.7 fusion.141
  150.3 171.6 %all-reduce.8.cloned.1.call-done = f32[16,4096]{1,0:T(8,128)} async-done(((f32[16,4096]{1,0:T(8,128)}), f32[16,4096]{1,0:T(8,128)}) %all-reduce.8.cloned.1.call-update) | async-done | bytes 262160 | tf_op jit(solution)/shard_map/psum | solution.py:144
  322.0 8.9 %fusion.201 = f32[16,4096]{1,0:T(8,128)S(1)} fusion(f32[16,4096]{1,0:T(8,128)S(1)} %copy-done.15, f32[16,4096]{1,0:T(8,128)} %all-reduce.8.cloned.1.call-done, f32[20,4100]{1,0:T(8,128)} %get-tuple-element.108, f32[20,4100]{1,0:T(8,128)} %get-tuple-element.106, f32[20,4100]{1,0:T(8,128)} %get-tuple-element.107, f32[20,4100]{1,0:T(8,128)} %get-tuple-element.86, ...), kind=kLoop, calls=%fused_computation.281 | loop fusion | flops 4915200 | bytes 13369344 | tf_op jit(solution)/shard_map/sub | solution.py:146
  332.8 2.4 collective-permute-start.4
  336.7 3.8 collective-permute-done.4
  340.8 2.7 fusion.66
  343.5 2.7 fusion.72
  346.2 5.6 fusion.304
  355.1 2.0 slice.650
  357.1 3.4 copy.101
  362.0 2.0 slice.649
  364.0 3.4 copy.100
  368.9 2.0 slice.648
  370.9 3.4 copy.99
  377.9 3.4 copy.98
  382.8 2.0 slice.646
  384.8 3.4 copy.97
  389.7 2.0 slice.645
  391.7 3.4 copy.96
  395.7 2.0 slice.644
  397.7 2.4 copy.95
  400.1 5.7 tanh_select_fusion
  405.8 2.1 copy.110
  407.9 2.7 concatenate.21.clone
  410.6 5.3 constant_dynamic-slice_fusion.6
  415.9 2.2 copy.108
  418.1 3.0 copy.107
  421.1 2.9 copy.106
  425.2 3.0 copy.104
  428.3 2.9 copy.103
  432.4 6.9 %fusion.247 = f32[16,4096]{1,0:T(8,128)} fusion(f32[16,4096]{1,0:T(8,128)S(1)} %copy.108, f32[16,4096]{1,0:T(8,128)} %copy.107, f32[16,4096]{1,0:T(8,128)} %copy.106, f32[16,4096]{1,0:T(8,128)} %copy.105, f32[16,4096]{1,0:T(8,128)} %copy.104, f32[16,4096]{1,0:T(8,128)} %copy.103, f32[16,4096]{1,0:T(8,128)} %copy.102, f32[]{:T(128)} %bitcast.7, ...), kind=kOutput, calls=%fused_computation.350 | convolution fusion | flops 13434880 | bytes 2100252 | tf_op jit(solution)/shard_map/while/body/eval_jaxpr/dot_general | solution.py:39
  439.4 2.7 fusion.69
  442.0 169.5 %all-reduce.10.cloned.1.call-done = f32[16,4096]{1,0:T(8,128)} async-done(((f32[16,4096]{1,0:T(8,128)}), f32[16,4096]{1,0:T(8,128)}) %all-reduce.10.cloned.1.call-update) | async-done | bytes 262160 | tf_op jit(solution)/shard_map/psum | solution.py:144
  611.6 9.6 %fusion.150 = f32[16,4096]{1,0:T(8,128)} fusion(f32[16,4096]{1,0:T(8,128)S(1)} %fusion.201, f32[16,4096]{1,0:T(8,128)} %all-reduce.10.cloned.1.call-done, f32[20,4100]{1,0:T(8,128)} %get-tuple-element.84, f32[20,4100]{1,0:T(8,128)} %get-tuple-element.82, f32[20,4100]{1,0:T(8,128)} %get-tuple-element.83, f32[20,4100]{1,0:T(8,128)} %get-tuple-element.62, ...), kind=kLoop, calls=%fused_computation.206 | loop fusion | flops 4915200 | bytes 13369344 | tf_op jit(solution)/shard_map/sub | solution.py:146
  (91 shorter events, 44.5 us)
Async XLA Ops:
  6.5 315.4 %all-reduce.8.cloned.1.call-start = ((), (), s32[]{:S(2)}) async-start(), calls=%async_computation | async-start | bytes 524288 | tf_op jit(solution)/shard_map/psum | solution.py:144
  6.5 43.0 %collective-permute-start.1 = (f32[16,4096]{1,0:T(8,128)}, f32[16,4096]{1,0:T(8,128)S(1)}, u32[]{:S(2)}, u32[]{:S(2)}) collective-permute-start(f32[16,4096]{1,0:T(8,128)} %param.4), channel_id=1, source_target_pairs={{16,0},{32,16},{48,32},{64,48},{80,64},{96,80},{112,96},{128,112},... | collective-permute-start | bytes 786440 | tf_op jit(solution)/shard_map/ppermute | solution.py:23
  8.5 41.1 %collective-permute-start = (f32[16,4096]{1,0:T(8,128)}, f32[16,4096]{1,0:T(8,128)S(1)}, u32[]{:S(2)}, u32[]{:S(2)}) collective-permute-start(f32[16,4096]{1,0:T(8,128)} %param.4), channel_id=1, source_target_pairs={{0,16},{16,32},{32,48},{48,64},{64,80},{80,96},{96,112},{112,128},... | collective-permute-start | bytes 786440 | tf_op jit(solution)/shard_map/ppermute | solution.py:20
  12.4 96.8 %collective-permute-start.3 = (f32[1,4,2048]{2,1,0:T(4,128)}, f32[1,4,2048]{2,1,0:T(4,128)}, u32[]{:S(2)}, u32[]{:S(2)}) collective-permute-start(f32[1,4,2048]{2,1,0:T(4,128)} %get-tuple-element.124), channel_id=1, source_target_pairs={{16,0},{32,16},{48,32},{64,48},{80,64},{96,80},{112,96},{128,112},... | collective-permute-start | bytes 98312 | tf_op jit(solution)/shard_map/ppermute | solution.py:23
  19.7 89.5 %collective-permute-start.2 = (f32[1,4,2048]{2,1,0:T(4,128)}, f32[1,4,2048]{2,1,0:T(4,128)}, u32[]{:S(2)}, u32[]{:S(2)}) collective-permute-start(f32[1,4,2048]{2,1,0:T(4,128)} %get-tuple-element.123), channel_id=1, source_target_pairs={{0,16},{16,32},{32,48},{48,64},{64,80},{80,96},{96,112},{112,128},... | collective-permute-start | bytes 98312 | tf_op jit(solution)/shard_map/ppermute | solution.py:20
  21.7 34.4 %copy-start.21 = (s32[16]{0:T(128)}, s32[16]{0:T(128)S(1)}, u32[]{:S(2)}) copy-start(s32[16]{0:T(128)S(1)} %iota_multiply_fusion) | copy-start | bytes 196
  53.4 2.7 copy-start.14
  104.8 4.5 copy-start.16
  104.8 4.5 copy-start.17
  104.8 4.5 copy-start.19
  104.8 4.5 copy-start.20
  126.8 5.2 copy-start.3
  133.3 5.9 copy-start.2
  147.4 174.6 %copy-start.9 = (f32[20,4100]{1,0:T(8,128)S(1)}, f32[20,4100]{1,0:T(8,128)}, u32[]{:S(2)}) copy-start(f32[20,4100]{1,0:T(8,128)} %get-tuple-element.101) | copy-start | bytes 984004
  147.4 174.6 %copy-start.10 = (f32[20,4100]{1,0:T(8,128)S(1)}, f32[20,4100]{1,0:T(8,128)}, u32[]{:S(2)}) copy-start(f32[20,4100]{1,0:T(8,128)} %get-tuple-element.102) | copy-start | bytes 984004
  147.4 174.6 %copy-start.11 = (f32[20,4100]{1,0:T(8,128)S(1)}, f32[20,4100]{1,0:T(8,128)}, u32[]{:S(2)}) copy-start(f32[20,4100]{1,0:T(8,128)} %get-tuple-element.103) | copy-start | bytes 984004
  147.4 174.6 %copy-start.12 = (f32[20,4100]{1,0:T(8,128)S(1)}, f32[20,4100]{1,0:T(8,128)}, u32[]{:S(2)}) copy-start(f32[20,4100]{1,0:T(8,128)} %get-tuple-element.104) | copy-start | bytes 984004
  147.4 174.6 %copy-start.13 = (f32[20,4100]{1,0:T(8,128)S(1)}, f32[20,4100]{1,0:T(8,128)}, u32[]{:S(2)}) copy-start(f32[20,4100]{1,0:T(8,128)} %get-tuple-element.105) | copy-start | bytes 984004
  147.4 174.6 %copy-start.15 = (f32[16,4096]{1,0:T(8,128)S(1)}, f32[16,4096]{1,0:T(8,128)}, u32[]{:S(2)}) copy-start(f32[16,4096]{1,0:T(8,128)} %param.4) | copy-start | bytes 786436
  147.4 464.2 %all-reduce.10.cloned.1.call-start = ((), (), s32[]{:S(2)}) async-start(), calls=%async_computation.1 | async-start | bytes 524288 | tf_op jit(solution)/shard_map/psum | solution.py:144
  330.9 5.8 collective-permute-start.5
  332.8 7.7 %collective-permute-start.4 = (f32[16,4096]{1,0:T(8,128)S(1)}, f32[16,4096]{1,0:T(8,128)S(1)}, u32[]{:S(2)}, u32[]{:S(2)}) collective-permute-start(f32[16,4096]{1,0:T(8,128)S(1)} %fusion.201), channel_id=1, source_target_pairs={{0,16},{16,32},{32,48},{48,64},{64,80},{80,96},{96,112},{112,128},... | collective-permute-start | bytes 786440 | tf_op jit(solution)/shard_map/ppermute | solution.py:20
  343.5 2.7 copy-start.22
  395.7 4.4 copy-start.18
  418.1 5.9 copy-start.1
  425.2 5.9 copy-start
  439.3 172.2 %copy-start.4 = (f32[20,4100]{1,0:T(8,128)S(1)}, f32[20,4100]{1,0:T(8,128)}, u32[]{:S(2)}) copy-start(f32[20,4100]{1,0:T(8,128)} %get-tuple-element.77) | copy-start | bytes 984004
  439.3 172.2 %copy-start.5 = (f32[20,4100]{1,0:T(8,128)S(1)}, f32[20,4100]{1,0:T(8,128)}, u32[]{:S(2)}) copy-start(f32[20,4100]{1,0:T(8,128)} %get-tuple-element.78) | copy-start | bytes 984004
  439.4 172.2 %copy-start.6 = (f32[20,4100]{1,0:T(8,128)S(1)}, f32[20,4100]{1,0:T(8,128)}, u32[]{:S(2)}) copy-start(f32[20,4100]{1,0:T(8,128)} %get-tuple-element.79) | copy-start | bytes 984004
  439.4 172.2 %copy-start.7 = (f32[20,4100]{1,0:T(8,128)S(1)}, f32[20,4100]{1,0:T(8,128)}, u32[]{:S(2)}) copy-start(f32[20,4100]{1,0:T(8,128)} %get-tuple-element.80) | copy-start | bytes 984004
  439.4 172.2 %copy-start.8 = (f32[20,4100]{1,0:T(8,128)S(1)}, f32[20,4100]{1,0:T(8,128)}, u32[]{:S(2)}) copy-start(f32[20,4100]{1,0:T(8,128)} %get-tuple-element.81) | copy-start | bytes 984004
Sparse Core Ops, SparseCore 0:
  147.5 174.4 all-reduce.7
  439.5 172.0 all-reduce.9
where the time goes:
time: 636 us; the launch traced here: 629 us
  waiting for transfers between devices  346 us (54%)
  local copies, waits for them, and re-layouts  151 us (24%)
  other arithmetic  55 us (9%)
  between operations  32.5 us (5%)
  matrix products  25.1 us (4%)
  starting transfers between devices  18.1 us (3%)
    psum x2, waiting for transfers between devices, local(): summed = lax.psum(data, 'frame')  341 us
    unnamed x76, local copies, waits for them, and re-layouts  81.7 us
    slice x14, local copies, waits for them, and re-layouts, add_frame(): pred = pred + taps[tap] * piece.reshape(low_rows, low_cols, FACTOR)[:, :, 0]  28.1 us
    dynamic_slice x16, local copies, waits for them, and re-layouts, add_frame(): piece = lax.dynamic_slice_in_dim(rows_done, start, FACTOR * low_cols, 1)  22.2 us
    sub x2, other arithmetic, local(): image = image - 0.1 * (summed + 0.05 * smooth)  18.6 us
    select_n x6, other arithmetic, prior_block(): slope = jnp.where(inside, jnp.tanh((centre - near) / 0.5), 0.0)  16 us
    dot_general x2, matrix products, contract(): lax.dot_general(left, right, (((left_dim,), (right_dim,)), ((), ())), pre...  13.8 us
  transfers between devices with their start and end apart: 8, of which 4 were waited for; matrix products, arithmetic and copies ran while one was open for 12% of the time, Pallas kernels for 0%

commit v1 on v0

v1 whole, which is shorter than its diff:
```python
import functools

import jax
import jax.numpy as jnp
from jax import lax
from jax.experimental import pallas as pl
from jax.experimental.pallas import tpu as pltpu
from jax.sharding import PartitionSpec as P

RADIUS = 3
TAPS = 2 * RADIUS + 1
WINDOW = 2
REACH = 8
OFFS = 2 * REACH + 1
SIDE = 4
CHUNK = 256
LOW = CHUNK // 2
EDGE = 12
ROWS = 16
BAND = 2 * ROWS
SPAN = 640
KDIM = 640
MESH = pl.DeviceIdType.MESH
F32 = jnp.float32
BF16 = jnp.bfloat16


def iota(shape, axis):
    return lax.broadcasted_iota(jnp.int32, shape, axis)


def three(value):
    high = value.astype(BF16)
    rest = value - high.astype(F32)
    middle = rest.astype(BF16)
    low = (rest - middle.astype(F32)).astype(BF16)
    return jnp.concatenate([high, middle, low], axis=0)


def pick(value, table):
    rows = value.shape[0]
    out = jnp.dot(three(value), table, preferred_element_type=F32)
    return out[:rows] + out[rows : 2 * rows] + out[2 * rows :]


def left(value, amount):
    width = value.shape[1]
    return value if amount % width == 0 else pltpu.roll(value, (-amount) % width, 1)


def kernel(
    tiles, est, frames, shifts, blur, out,
    xw, fr, ys, yb, fb, sb, xs, px, pg, xb, aa, af, hh, d1, r1, d2, r2, pr,
    load_sem, ysend, yrecv, hsend, hrecv, fsend, frecv, ssend, srecv,
    e1send, e1recv, e2send, e2recv, gsend, grecv,
):
    t = lax.axis_index("tile")
    f = lax.axis_index("frame")
    x = f // SIDE
    y = f % SIDE
    c = SIDE * y + x
    last = SIDE * SIDE - 1
    at_low = (last - c) // last
    at_high = c // last
    start = pl.multiple_of(128 * (2 * c - 1 + at_low - at_high), 128)
    lane0 = pl.multiple_of(128 * (1 + at_low - at_high), 128)
    up = lax.rem(t + tiles - 1, tiles)
    down = lax.rem(t + 1, tiles)

    def ypeer(e):
        return {"frame": SIDE * x + lax.rem(y + e, SIDE)}

    def xpeer(e):
        return {"frame": SIDE * lax.rem(x + e, SIDE) + y}

    def remote(src, dst, send, recv, device):
        return pltpu.make_async_remote_copy(
            src_ref=src, dst_ref=dst, send_sem=send, recv_sem=recv, device_id=device, device_id_type=MESH
        )

    window = est.at[:, pl.ds(start, 512)]
    load_f = pltpu.make_async_copy(frames.at[0], fr, load_sem.at[0])
    load_x = pltpu.make_async_copy(window, xw.at[pl.ds(ROWS, ROWS), pl.ds(lane0, 512)], load_sem.at[1])
    load_f.start()
    load_x.start()

    barrier = pltpu.get_barrier_semaphore()
    for e in range(1, SIDE):
        pl.semaphore_signal(barrier, inc=1, device_id=ypeer(e), device_id_type=MESH)
        pl.semaphore_signal(barrier, inc=1, device_id=xpeer(e), device_id_type=MESH)
    pl.semaphore_signal(barrier, inc=1, device_id={"tile": up}, device_id_type=MESH)
    pl.semaphore_signal(barrier, inc=1, device_id={"tile": down}, device_id_type=MESH)

    load_f.wait()
    lane = iota((8, 128), 1)
    sub = iota((8, 128), 0)
    shift_tile = jnp.where(
        sub < 4, jnp.full((8, 128), shifts[0, 0].astype(F32)), jnp.full((8, 128), shifts[0, 1].astype(F32))
    )
    before = jnp.zeros((8, 128), F32)
    per_span = SIDE * LOW // 128
    for tile in range(SIDE * per_span + 1):
        if tile < SIDE * per_span:
            rolled = pltpu.roll(fr[:, 128 * tile : 128 * tile + 128], EDGE, 1)
        else:
            rolled = jnp.zeros((8, 128), F32)
        moved = jnp.where(lane < EDGE, before, rolled)
        before = rolled
        if tile < SIDE * per_span:
            at = 128 * (tile % per_span)
            ys[tile // per_span, :, at : at + 128] = moved
        if tile and tile % per_span == 0:
            ys[tile // per_span - 1, :, SPAN - 128 : SPAN] = jnp.where(lane < 2 * EDGE, moved, shift_tile)
    yb[0] = ys[y]

    pl.semaphore_wait(barrier, 2 * SIDE)

    started = []

    def go(copy):
        copy.start()
        started.append(copy)
        return copy

    ycopies = {}
    for e in (2, 1, 3):
        target = lax.rem(y + e, SIDE)
        ycopies[e] = go(remote(ys.at[target], yb.at[e], ysend.at[e], yrecv.at[e], ypeer(e)))
    halo_down = go(
        remote(window, xw.at[pl.ds(0, ROWS), pl.ds(lane0, 512)], hsend.at[0], hrecv.at[0], {"tile": down})
    )
    halo_up = go(
        remote(window, xw.at[pl.ds(2 * ROWS, ROWS), pl.ds(lane0, 512)], hsend.at[1], hrecv.at[1], {"tile": up})
    )
    fcopies = {}
    scopies = {}

    def forward(ey):
        for ex in (2, 1, 3):
            target = pl.multiple_of(LOW * lax.rem(x + ex, SIDE), LOW)
            slot = SIDE * ex + ey
            scopies[slot] = go(
                remote(yb.at[ey, :, pl.ds(SPAN - 128, 128)], sb.at[ex, ey], ssend.at[slot], srecv.at[slot], xpeer(ex))
            )
            fcopies[slot] = go(
                remote(yb.at[ey, :, pl.ds(target, 256)], fb.at[ex, ey], fsend.at[slot], frecv.at[slot], xpeer(ex))
            )
        fb[0, ey] = yb[ey, :, pl.ds(pl.multiple_of(LOW * x, LOW), 256)]
        sb[0, ey] = yb[ey, :, pl.ds(SPAN - 128, 128)]

    forward(0)

    high_cols = CHUNK * SIDE * SIDE
    load_x.wait()
    halo_down.wait_recv()
    halo_up.wait_recv()
    row = ROWS * t - ROWS + iota((3 * ROWS, 512), 0)
    col = CHUNK * c - 128 + iota((3 * ROWS, 512), 1)
    inside = (row >= 0) & (row < ROWS * tiles) & (col >= 0) & (col < high_cols)
    raw = jnp.where(inside, xw[:, 128:640], 0.0)
    lane_in = iota((512, 256), 0)
    lane_out = iota((512, 256), 1)
    for phase in range(2):
        table = jnp.where(lane_in == 96 + phase + 2 * lane_out, 1.0, 0.0).astype(BF16)
        xs[phase] = pick(raw, table)

    row = ROWS * t - ROWS + iota((3 * ROWS, 256), 0)
    col = CHUNK * c - 32 + 2 * iota((3 * ROWS, 256), 1)
    inside = (row >= 0) & (row < ROWS * tiles) & (col >= 0) & (col < high_cols)
    gain = jnp.where(inside, 2.0, 1.0)
    pg[0] = left(gain, -1)
    pg[1] = gain
    pg[2] = left(gain, 1)

    def stage_model(lo):
        for off in range(OFFS):
            xb[BAND * off : BAND * off + BAND] = left(xs[off % 2, lo : lo + BAND], off // 2)

    def stage_prior(lo, count):
        for phase in range(2):
            double = 2.0 * xs[phase, lo : lo + count]
            px[3 * phase, lo : lo + count] = left(double, -1)
            px[3 * phase + 1, lo : lo + count] = double
            px[3 * phase + 2, lo : lo + count] = left(double, 1)

    def prior(phase, lo, count):
        centre = px[3 * phase + 1, lo : lo + count]
        total = jnp.zeros((count, 256), F32)
        for side in range(-WINDOW, WINDOW + 1):
            other = (phase + side) % 2
            lanes = (phase + side - other) // 2 + 1
            for down_off in range(-WINDOW, WINDOW + 1):
                if down_off == 0 and side == 0:
                    continue
                rows = slice(lo + down_off, lo + down_off + count)
                weight = 0.7 ** (abs(down_off) + abs(side))
                slope = jnp.tanh(centre - px[3 * other + lanes, rows])
                total = total + (weight * slope) * pg[lanes, rows]
        return total

    xb[OFFS * BAND : KDIM] = jnp.zeros((KDIM - OFFS * BAND, 256), F32)
    aa[OFFS * BAND : KDIM] = jnp.zeros((KDIM - OFFS * BAND, 128), F32)
    stage_model(REACH)
    stage_prior(0, 3 * ROWS)

    for ey in (1, 3, 2):
        ycopies[ey].wait_recv()
        forward(ey)

    for phase in range(2):
        pr[phase] = xs[phase, REACH : REACH + BAND] - 0.005 * prior(phase, REACH, BAND)

    for copy in scopies.values():
        copy.wait_recv()
    tile = jnp.zeros((8, 128), F32)
    for slot in range(SIDE * SIDE):
        piece = sb[slot // SIDE, slot % SIDE]
        if slot < 3:
            piece = pltpu.roll(piece, 64, 1)
        tile = jnp.where(lane // 8 == slot, piece, tile)
    blur_sum = blur[0]
    for tap in range(1, TAPS):
        blur_sum = blur_sum + blur[tap]
    scale = jnp.full((1, 128), blur_sum)
    taps = [jnp.full((1, 128), blur[tap]) / scale for tap in range(TAPS)]

    def tap_at(distance):
        total = jnp.zeros(distance.shape, F32)
        for tap in range(TAPS):
            total = jnp.where(distance == float(tap - RADIUS), jnp.broadcast_to(taps[tap], distance.shape), total)
        return total

    place = (iota((BAND, 128), 0) - REACH - 2 * (iota((BAND, 128), 1) % 8)).astype(F32)
    by_row = tap_at(place - tile[0:1])
    by_col = tap_at((iota((24, 128), 0) - REACH).astype(F32) - tile[4:5])
    for off in range(OFFS):
        aa[BAND * off : BAND * off + BAND] = by_row * by_col[off : off + 1]
    for block in range(KDIM // 128):
        af[:, 128 * block : 128 * block + 128] = aa[128 * block : 128 * block + 128].T

    low = LOW * c - EDGE + iota((128, 256), 1)
    live = (low >= 0) & (low < LOW * SIDE * SIDE)

    def misfits():
        pred = jnp.dot(af[...], xb[...], precision=lax.Precision.HIGH, preferred_element_type=F32)
        return pred

    def adjoint(pred):
        gap = jnp.where(live, jnp.tanh(pred - fb[...].reshape(128, 256)), 0.0)
        hh[...] = jnp.dot(
            aa[: OFFS * BAND], gap, precision=lax.Precision.HIGH, preferred_element_type=F32
        )

    pred = misfits()
    for copy in fcopies.values():
        copy.wait_recv()
    adjoint(pred)
    for phase in range(2):
        total = jnp.zeros((BAND, 256), F32)
        for off in range(phase, OFFS, 2):
            total = total + left(hh[BAND * off : BAND * off + BAND], -(off // 2))
        d1[phase] = total
    to_up = go(remote(d1.at[:, pl.ds(0, ROWS)], r1.at[:, pl.ds(ROWS, ROWS)], e1send.at[0], e1recv.at[0], {"tile": up}))
    to_down = go(
        remote(d1.at[:, pl.ds(ROWS, ROWS)], r1.at[:, pl.ds(0, ROWS)], e1send.at[1], e1recv.at[1], {"tile": down})
    )
    reach_row = ROWS * t - REACH + iota((BAND, 256), 0)
    edge_row = (reach_row < REACH) | (reach_row >= ROWS * tiles - REACH)
    within = pg[1, REACH : REACH + BAND] > 1.5
    to_up.wait_recv()
    to_down.wait_recv()
    for phase in range(2):
        theirs = jnp.where(edge_row, 0.0, r1[phase])
        xs[phase, REACH : REACH + BAND] = jnp.where(within, pr[phase] - 0.1 * (d1[phase] + theirs), 0.0)

    stage_model(REACH)
    adjoint(misfits())
    both = []
    for phase in range(2):
        total = jnp.zeros((BAND, 128), F32)
        for off in range(phase, OFFS, 2):
            total = total + left(hh[BAND * off : BAND * off + BAND], ROWS - off // 2)[:, :128]
        d2[0, phase] = total[:REACH]
        d2[1, phase] = total[3 * REACH :]
        both.append(total[REACH : 3 * REACH])
    to_up2 = go(remote(d2.at[0], r2.at[1], e2send.at[0], e2recv.at[0], {"tile": up}))
    to_down2 = go(remote(d2.at[1], r2.at[0], e2send.at[1], e2recv.at[1], {"tile": down}))

    stage_prior(REACH, BAND)
    for phase in range(2):
        mine = xs[phase, ROWS : 2 * ROWS] - 0.005 * prior(phase, ROWS, ROWS)
        both[phase] = left(mine, ROWS)[:, :128] - 0.1 * both[phase]
    lane_in = iota((CHUNK, CHUNK), 0)
    lane_out = iota((CHUNK, CHUNK), 1)
    table = jnp.where(lane_out == jnp.where(lane_in < LOW, 2 * lane_in, 2 * lane_in - CHUNK + 1), 1.0, 0.0).astype(BF16)
    own_row = ROWS * t + iota((ROWS, LOW), 0)
    edge_row = (own_row < REACH) | (own_row >= ROWS * tiles - REACH)
    to_up2.wait_recv()
    to_down2.wait_recv()
    halves = []
    for phase in range(2):
        theirs = jnp.concatenate([r2[0, phase], r2[1, phase]], axis=0)
        halves.append(both[phase] - 0.1 * jnp.where(edge_row, 0.0, theirs))
    result = pick(jnp.concatenate(halves, axis=1), table)

    def chunk_of(ey):
        source = SIDE * lax.rem(y + SIDE - ey, SIDE) + x
        return out.at[:, pl.ds(pl.multiple_of(CHUNK * source, CHUNK), CHUNK)]

    out[:, pl.ds(pl.multiple_of(CHUNK * c, CHUNK), CHUNK)] = result
    gathers = {}
    for e in (2, 1, 3):
        gathers[e] = go(remote(chunk_of(0), chunk_of(0), gsend.at[e], grecv.at[e], ypeer(e)))

    def spread(ey):
        for ex in (2, 1, 3):
            slot = SIDE * ex + ey
            gathers[slot] = go(remote(chunk_of(ey), chunk_of(ey), gsend.at[slot], grecv.at[slot], xpeer(ex)))

    spread(0)
    for ey in (1, 3, 2):
        gathers[ey].wait_recv()
        spread(ey)
    for slot, copy in gathers.items():
        if slot >= SIDE:
            copy.wait_recv()
    for copy in started:
        copy.wait_send()


def local(tiles, estimate, frames, shifts, blur):
    vmem = lambda *shape: pltpu.VMEM(shape, F32)
    dma = lambda n: pltpu.SemaphoreType.DMA((n,))
    both = SIDE * SIDE
    return pl.pallas_call(
        functools.partial(kernel, tiles),
        out_shape=jax.ShapeDtypeStruct(estimate.shape, F32),
        in_specs=[
            pl.BlockSpec(memory_space=pl.ANY),
            pl.BlockSpec(memory_space=pl.ANY),
            pl.BlockSpec(memory_space=pltpu.SMEM),
            pl.BlockSpec(memory_space=pltpu.SMEM),
        ],
        out_specs=pl.BlockSpec(memory_space=pltpu.VMEM),
        scratch_shapes=[
            vmem(3 * ROWS, 768),
            vmem(8, SIDE * SIDE * LOW),
            vmem(SIDE, 8, SPAN),
            vmem(SIDE, 8, SPAN),
            vmem(SIDE, SIDE, 8, 256),
            vmem(SIDE, SIDE, 8, 128),
            vmem(2, 3 * ROWS, 256),
            vmem(6, 3 * ROWS, 256),
            vmem(3, 3 * ROWS, 256),
            vmem(KDIM, 256),
            vmem(KDIM, 128),
            vmem(128, KDIM),
            vmem(OFFS * BAND, 256),
            vmem(2, BAND, 256),
            vmem(2, BAND, 256),
            vmem(2, 2, REACH, 128),
            vmem(2, 2, REACH, 128),
            vmem(2, BAND, 256),
            dma(2), dma(SIDE), dma(SIDE), dma(2), dma(2), dma(both), dma(both), dma(both), dma(both),
            dma(2), dma(2), dma(2), dma(2), dma(both), dma(both),
        ],
        compiler_params=pltpu.CompilerParams(collective_id=0, has_side_effects=True),
    )(estimate, frames, shifts, blur)


def solution(mesh):
    placed = (P("tile", None), P("frame", "tile", None), P("frame", None), P())
    return jax.shard_map(
        functools.partial(local, mesh.shape["tile"]),
        mesh=mesh, in_specs=placed, out_specs=P("tile", None), check_vma=False,
    )
```

time: 636 us -> 43 us (0.07)
  the two profiles are of different devices: /device:TPU:8 before, /device:TPU:16 now
where the time goes in v1:
time: 43 us; the launch traced here: 42.8 us
  Pallas kernels  41.1 us (96%)
  local copies, waits for them, and re-layouts  1.67 us (4%)
    pallas_call x1, Pallas kernels, local(): pl.pallas_call(functools.partial(kernel, tiles), out_shape=jax.ShapeDtype...  41.1 us
    unnamed x1, local copies, waits for them, and re-layouts  1.67 us

profile of v1, /device:TPU:16, one launch (start us, length us, event | category | flops | bytes accessed | tf_op | source)
XLA Modules:
  0.0 42.8 jit_solution(17042900606628508179)
XLA Ops:
  0.0 41.1 %shard_map.46 = f32[16,4096]{1,0:T(8,128)} custom-call(f32[16,4096]{1,0:T(8,128)} %est.1, f32[1,8,2048]{2,1,0:T(8,128)} %frames.1, s32[1,2]{1,0:T(1,128)} %shifts.1, f32[7]{0:T(128)} %blur.1), custom_call_target="tpu_custom_call" | custom-call | tf_op jit(solution)/shard_map/pallas_call | solution.py:335
  41.1 1.7 %copy.6 = f32[16,4096]{1,0:T(8,128)} copy(f32[16,4096]{1,0:T(8,128)} %shard_map.46) | data formatting | bytes 524288

commit v2 on v1

--- a/solution.py
+++ b/solution.py
@@ -18,7 +18,8 @@
 EDGE = 12
 ROWS = 16
 BAND = 2 * ROWS
-SPAN = 640
+SPAN = 768
+PIECE = 384
 KDIM = 640
 MESH = pl.DeviceIdType.MESH
 F32 = jnp.float32
@@ -50,8 +51,8 @@
 
 def kernel(
     tiles, est, frames, shifts, blur, out,
-    xw, fr, ys, yb, fb, sb, xs, px, pg, xb, aa, af, hh, d1, r1, d2, r2, pr,
-    load_sem, ysend, yrecv, hsend, hrecv, fsend, frecv, ssend, srecv,
+    taps_in, xw, yb, fb, fs, sy, sx, xs, px, pg, xb, aa, af, hh, d1, r1, d2, r2, pr,
+    load_sem, ysend, yrecv, hsend, hrecv, fsend, frecv, usend, urecv, ssend, srecv,
     e1send, e1recv, e2send, e2recv, gsend, grecv,
 ):
     t = lax.axis_index("tile")
@@ -78,42 +79,52 @@
             src_ref=src, dst_ref=dst, send_sem=send, recv_sem=recv, device_id=device, device_id_type=MESH
         )
 
+    def across_tiles(above, below):
+        has_above, has_below = t > 0, t < tiles - 1
+
+        class Pair:
+            def start(self):
+                pl.when(has_above)(above.start)
+                pl.when(has_below)(below.start)
+
+            def wait_recv(self):
+                pl.when(has_above)(below.wait_recv)
+                pl.when(has_below)(above.wait_recv)
+
+            def wait_send(self):
+                pl.when(has_above)(above.wait_send)
+                pl.when(has_below)(below.wait_send)
+
+        return Pair()
+
+    def span(target):
+        edge = (SIDE - 1 - target) // (SIDE - 1) - target // (SIDE - 1)
+        source = pl.multiple_of(128 * (SIDE * target - 1 + edge), 128)
+        return frames.at[0, :, pl.ds(source, SPAN)], pl.ds(pl.multiple_of(128 * (1 + edge), 128), SPAN)
+
     window = est.at[:, pl.ds(start, 512)]
-    load_f = pltpu.make_async_copy(frames.at[0], fr, load_sem.at[0])
+    own_span, own_lanes = span(y)
+    load_f = pltpu.make_async_copy(own_span, yb.at[0, :, own_lanes], load_sem.at[0])
     load_x = pltpu.make_async_copy(window, xw.at[pl.ds(ROWS, ROWS), pl.ds(lane0, 512)], load_sem.at[1])
+    load_s = pltpu.make_async_copy(shifts, sy.at[0], load_sem.at[2])
+    load_b = pltpu.make_async_copy(blur, taps_in, load_sem.at[3])
+
+    barrier = pltpu.get_barrier_semaphore()
+
+    def greet(device):
+        pl.semaphore_signal(barrier, inc=1, device_id=device, device_id_type=MESH)
+
+    for e in (2, 1, 3):
+        greet(ypeer(e))
+    for e in (2, 1, 3):
+        greet(xpeer(e))
+    pl.when(t > 0)(lambda: greet({"tile": up}))
+    pl.when(t < tiles - 1)(lambda: greet({"tile": down}))
     load_f.start()
     load_x.start()
-
-    barrier = pltpu.get_barrier_semaphore()
-    for e in range(1, SIDE):
-        pl.semaphore_signal(barrier, inc=1, device_id=ypeer(e), device_id_type=MESH)
-        pl.semaphore_signal(barrier, inc=1, device_id=xpeer(e), device_id_type=MESH)
-    pl.semaphore_signal(barrier, inc=1, device_id={"tile": up}, device_id_type=MESH)
-    pl.semaphore_signal(barrier, inc=1, device_id={"tile": down}, device_id_type=MESH)
-
-    load_f.wait()
-    lane = iota((8, 128), 1)
-    sub = iota((8, 128), 0)
-    shift_tile = jnp.where(
-        sub < 4, jnp.full((8, 128), shifts[0, 0].astype(F32)), jnp.full((8, 128), shifts[0, 1].astype(F32))
-    )
-    before = jnp.zeros((8, 128), F32)
-    per_span = SIDE * LOW // 128
-    for tile in range(SIDE * per_span + 1):
-        if tile < SIDE * per_span:
-            rolled = pltpu.roll(fr[:, 128 * tile : 128 * tile + 128], EDGE, 1)
-        else:
-            rolled = jnp.zeros((8, 128), F32)
-        moved = jnp.where(lane < EDGE, before, rolled)
-        before = rolled
-        if tile < SIDE * per_span:
-            at = 128 * (tile % per_span)
-            ys[tile // per_span, :, at : at + 128] = moved
-        if tile and tile % per_span == 0:
-            ys[tile // per_span - 1, :, SPAN - 128 : SPAN] = jnp.where(lane < 2 * EDGE, moved, shift_tile)
-    yb[0] = ys[y]
-
-    pl.semaphore_wait(barrier, 2 * SIDE)
+    load_s.start()
+    load_b.start()
+    pl.semaphore_wait(barrier, 2 * SIDE - 1 + (t + tiles - 1) // tiles - (t + 1) // tiles)
 
     started = []
 
@@ -123,37 +134,36 @@
         return copy
 
     ycopies = {}
+    ucopies = {}
     for e in (2, 1, 3):
-        target = lax.rem(y + e, SIDE)
-        ycopies[e] = go(remote(ys.at[target], yb.at[e], ysend.at[e], yrecv.at[e], ypeer(e)))
-    halo_down = go(
-        remote(window, xw.at[pl.ds(0, ROWS), pl.ds(lane0, 512)], hsend.at[0], hrecv.at[0], {"tile": down})
-    )
-    halo_up = go(
-        remote(window, xw.at[pl.ds(2 * ROWS, ROWS), pl.ds(lane0, 512)], hsend.at[1], hrecv.at[1], {"tile": up})
+        source, lanes = span(lax.rem(y + e, SIDE))
+        ucopies[e] = go(remote(shifts, sy.at[e], usend.at[e], urecv.at[e], ypeer(e)))
+        ycopies[e] = go(remote(source, yb.at[e, :, lanes], ysend.at[e], yrecv.at[e], ypeer(e)))
+    halo = go(
+        across_tiles(
+            remote(window, xw.at[pl.ds(2 * ROWS, ROWS), pl.ds(lane0, 512)], hsend.at[0], hrecv.at[1], {"tile": up}),
+            remote(window, xw.at[pl.ds(0, ROWS), pl.ds(lane0, 512)], hsend.at[1], hrecv.at[0], {"tile": down}),
+        )
     )
     fcopies = {}
     scopies = {}
 
     def forward(ey):
         for ex in (2, 1, 3):
-            target = pl.multiple_of(LOW * lax.rem(x + ex, SIDE), LOW)
+            target = pl.multiple_of(LOW * lax.rem(x + ex, SIDE) + 128, 128)
             slot = SIDE * ex + ey
-            scopies[slot] = go(
-                remote(yb.at[ey, :, pl.ds(SPAN - 128, 128)], sb.at[ex, ey], ssend.at[slot], srecv.at[slot], xpeer(ex))
+            scopies[slot] = go(remote(sy.at[ey], sx.at[ex, ey], ssend.at[slot], srecv.at[slot], xpeer(ex)))
+            fcopies[slot] = go(
+                remote(yb.at[ey, :, pl.ds(target, PIECE)], fb.at[ex, ey], fsend.at[slot], frecv.at[slot], xpeer(ex))
             )
-            fcopies[slot] = go(
-                remote(yb.at[ey, :, pl.ds(target, 256)], fb.at[ex, ey], fsend.at[slot], frecv.at[slot], xpeer(ex))
-            )
-        fb[0, ey] = yb[ey, :, pl.ds(pl.multiple_of(LOW * x, LOW), 256)]
-        sb[0, ey] = yb[ey, :, pl.ds(SPAN - 128, 128)]
-
+
+    load_f.wait()
+    load_s.wait()
     forward(0)
 
     high_cols = CHUNK * SIDE * SIDE
     load_x.wait()
-    halo_down.wait_recv()
-    halo_up.wait_recv()
+    halo.wait_recv()
     row = ROWS * t - ROWS + iota((3 * ROWS, 512), 0)
     col = CHUNK * c - 128 + iota((3 * ROWS, 512), 1)
     inside = (row >= 0) & (row < ROWS * tiles) & (col >= 0) & (col < high_cols)
@@ -204,6 +214,7 @@
     stage_prior(0, 3 * ROWS)
 
     for ey in (1, 3, 2):
+        ucopies[ey].wait_recv()
         ycopies[ey].wait_recv()
         forward(ey)
 
@@ -212,27 +223,30 @@
 
     for copy in scopies.values():
         copy.wait_recv()
-    tile = jnp.zeros((8, 128), F32)
+    frame = iota((1, 128), 1) // 8
+    down_shift = jnp.zeros((1, 128), jnp.int32)
+    side_shift = jnp.zeros((1, 128), jnp.int32)
     for slot in range(SIDE * SIDE):
-        piece = sb[slot // SIDE, slot % SIDE]
-        if slot < 3:
-            piece = pltpu.roll(piece, 64, 1)
-        tile = jnp.where(lane // 8 == slot, piece, tile)
-    blur_sum = blur[0]
+        ex, ey = slot // SIDE, slot % SIDE
+        pair = sx[ex, ey] if ex else sy[ey]
+        down_shift = jnp.where(frame == slot, pair[0:1, 0:1], down_shift)
+        side_shift = jnp.where(frame == slot, pair[0:1, 1:2], side_shift)
+    load_b.wait()
+    blur_sum = taps_in[0]
     for tap in range(1, TAPS):
-        blur_sum = blur_sum + blur[tap]
+        blur_sum = blur_sum + taps_in[tap]
     scale = jnp.full((1, 128), blur_sum)
-    taps = [jnp.full((1, 128), blur[tap]) / scale for tap in range(TAPS)]
+    taps = [jnp.full((1, 128), taps_in[tap]) / scale for tap in range(TAPS)]
 
     def tap_at(distance):
         total = jnp.zeros(distance.shape, F32)
         for tap in range(TAPS):
-            total = jnp.where(distance == float(tap - RADIUS), jnp.broadcast_to(taps[tap], distance.shape), total)
+            total = jnp.where(distance == tap - RADIUS, jnp.broadcast_to(taps[tap], distance.shape), total)
         return total
 
-    place = (iota((BAND, 128), 0) - REACH - 2 * (iota((BAND, 128), 1) % 8)).astype(F32)
-    by_row = tap_at(place - tile[0:1])
-    by_col = tap_at((iota((24, 128), 0) - REACH).astype(F32) - tile[4:5])
+    place = iota((BAND, 128), 0) - REACH - 2 * (iota((BAND, 128), 1) % 8)
+    by_row = tap_at(place - down_shift)
+    by_col = tap_at(iota((24, 128), 0) - REACH - side_shift)
     for off in range(OFFS):
         aa[BAND * off : BAND * off + BAND] = by_row * by_col[off : off + 1]
     for block in range(KDIM // 128):
@@ -246,29 +260,36 @@
         return pred
 
     def adjoint(pred):
-        gap = jnp.where(live, jnp.tanh(pred - fb[...].reshape(128, 256)), 0.0)
+        gap = jnp.where(live, jnp.tanh(pred - fs[...]), 0.0)
         hh[...] = jnp.dot(
             aa[: OFFS * BAND], gap, precision=lax.Precision.HIGH, preferred_element_type=F32
         )
 
     pred = misfits()
-    for copy in fcopies.values():
-        copy.wait_recv()
+    for slot in range(SIDE * SIDE):
+        ex, ey = slot // SIDE, slot % SIDE
+        if ex:
+            fcopies[slot].wait_recv()
+            piece = fb[ex, ey]
+        else:
+            piece = yb[ey, :, pl.ds(pl.multiple_of(LOW * x + 128, 128), PIECE)]
+        fs[8 * slot : 8 * slot + 8] = left(piece, 128 - EDGE)[:, :256]
     adjoint(pred)
     for phase in range(2):
         total = jnp.zeros((BAND, 256), F32)
         for off in range(phase, OFFS, 2):
             total = total + left(hh[BAND * off : BAND * off + BAND], -(off // 2))
         d1[phase] = total
-    to_up = go(remote(d1.at[:, pl.ds(0, ROWS)], r1.at[:, pl.ds(ROWS, ROWS)], e1send.at[0], e1recv.at[0], {"tile": up}))
-    to_down = go(
-        remote(d1.at[:, pl.ds(ROWS, ROWS)], r1.at[:, pl.ds(0, ROWS)], e1send.at[1], e1recv.at[1], {"tile": down})
+    first = go(
+        across_tiles(
+            remote(d1.at[:, pl.ds(0, ROWS)], r1.at[:, pl.ds(ROWS, ROWS)], e1send.at[0], e1recv.at[1], {"tile": up}),
+            remote(d1.at[:, pl.ds(ROWS, ROWS)], r1.at[:, pl.ds(0, ROWS)], e1send.at[1], e1recv.at[0], {"tile": down}),
+        )
     )
     reach_row = ROWS * t - REACH + iota((BAND, 256), 0)
     edge_row = (reach_row < REACH) | (reach_row >= ROWS * tiles - REACH)
     within = pg[1, REACH : REACH + BAND] > 1.5
-    to_up.wait_recv()
-    to_down.wait_recv()
+    first.wait_recv()
     for phase in range(2):
         theirs = jnp.where(edge_row, 0.0, r1[phase])
         xs[phase, REACH : REACH + BAND] = jnp.where(within, pr[phase] - 0.1 * (d1[phase] + theirs), 0.0)
@@ -283,8 +304,12 @@
         d2[0, phase] = total[:REACH]
         d2[1, phase] = total[3 * REACH :]
         both.append(total[REACH : 3 * REACH])
-    to_up2 = go(remote(d2.at[0], r2.at[1], e2send.at[0], e2recv.at[0], {"tile": up}))
-    to_down2 = go(remote(d2.at[1], r2.at[0], e2send.at[1], e2recv.at[1], {"tile": down}))
+    second = go(
+        across_tiles(
+            remote(d2.at[0], r2.at[1], e2send.at[0], e2recv.at[1], {"tile": up}),
+            remote(d2.at[1], r2.at[0], e2send.at[1], e2recv.at[0], {"tile": down}),
+        )
+    )
 
     stage_prior(REACH, BAND)
     for phase in range(2):
@@ -295,8 +320,7 @@
     table = jnp.where(lane_out == jnp.where(lane_in < LOW, 2 * lane_in, 2 * lane_in - CHUNK + 1), 1.0, 0.0).astype(BF16)
     own_row = ROWS * t + iota((ROWS, LOW), 0)
     edge_row = (own_row < REACH) | (own_row >= ROWS * tiles - REACH)
-    to_up2.wait_recv()
-    to_down2.wait_recv()
+    second.wait_recv()
     halves = []
     for phase in range(2):
         theirs = jnp.concatenate([r2[0, phase], r2[1, phase]], axis=0)
@@ -335,20 +359,16 @@
     return pl.pallas_call(
         functools.partial(kernel, tiles),
         out_shape=jax.ShapeDtypeStruct(estimate.shape, F32),
-        in_specs=[
-            pl.BlockSpec(memory_space=pl.ANY),
-            pl.BlockSpec(memory_space=pl.ANY),
-            pl.BlockSpec(memory_space=pltpu.SMEM),
-            pl.BlockSpec(memory_space=pltpu.SMEM),
-        ],
+        in_specs=[pl.BlockSpec(memory_space=pl.ANY)] * 4,
         out_specs=pl.BlockSpec(memory_space=pltpu.VMEM),
         scratch_shapes=[
+            pltpu.SMEM((TAPS,), F32),
             vmem(3 * ROWS, 768),
-            vmem(8, SIDE * SIDE * LOW),
-            vmem(SIDE, 8, SPAN),
-            vmem(SIDE, 8, SPAN),
-            vmem(SIDE, SIDE, 8, 256),
-            vmem(SIDE, SIDE, 8, 128),
+            vmem(SIDE, 8, SPAN + 256),
+            vmem(SIDE, SIDE, 8, PIECE),
+            vmem(128, 256),
+            pltpu.VMEM((SIDE, 1, 2), jnp.int32),
+            pltpu.VMEM((SIDE, SIDE, 1, 2), jnp.int32),
             vmem(2, 3 * ROWS, 256),
             vmem(6, 3 * ROWS, 256),
             vmem(3, 3 * ROWS, 256),
@@ -361,7 +381,7 @@
             vmem(2, 2, REACH, 128),
             vmem(2, 2, REACH, 128),
             vmem(2, BAND, 256),
-            dma(2), dma(SIDE), dma(SIDE), dma(2), dma(2), dma(both), dma(both), dma(both), dma(both),
+            dma(4), dma(SIDE), dma(SIDE), dma(2), dma(2), dma(both), dma(both), dma(SIDE), dma(SIDE), dma(both), dma(both),
             dma(2), dma(2), dma(2), dma(2), dma(both), dma(both),
         ],
         compiler_params=pltpu.CompilerParams(collective_id=0, has_side_effects=True),

time: 43 us -> 38.6 us (0.90)
  the two profiles are of different devices: /device:TPU:16 before, /device:TPU:256 now
where the time goes in v2:
time: 38.6 us; the launch traced here: 38.4 us
  Pallas kernels  36.7 us (95%)
  local copies, waits for them, and re-layouts  1.67 us (4%)
    pallas_call x1, Pallas kernels, local(): pl.pallas_call(functools.partial(kernel, tiles), out_shape=jax.ShapeDtype...  36.7 us
    unnamed x1, local copies, waits for them, and re-layouts  1.67 us

profile of v2, /device:TPU:256, one launch (start us, length us, event | category | flops | bytes accessed | tf_op | source)
XLA Modules:
  0.0 38.4 jit_solution(11807039867389747978)
XLA Ops:
  0.0 36.7 %shard_map.46 = f32[16,4096]{1,0:T(8,128)} custom-call(f32[16,4096]{1,0:T(8,128)} %est.1, f32[1,8,2048]{2,1,0:T(8,128)} %frames.1, s32[1,2]{1,0:T(1,128)} %shifts.1, f32[7]{0:T(128)} %blur.1), custom_call_target="tpu_custom_call" | custom-call | tf_op jit(solution)/shard_map/pallas_call | solution.py:359
  36.7 1.7 %copy.6 = f32[16,4096]{1,0:T(8,128)} copy(f32[16,4096]{1,0:T(8,128)} %shard_map.46) | data formatting | bytes 524288

commit v3 on v2

--- a/solution.py
+++ b/solution.py
@@ -18,8 +18,8 @@
 EDGE = 12
 ROWS = 16
 BAND = 2 * ROWS
-SPAN = 768
-PIECE = 384
+PIECE = 256
+FRAMES = SIDE * SIDE
 KDIM = 640
 MESH = pl.DeviceIdType.MESH
 F32 = jnp.float32
@@ -51,8 +51,8 @@
 
 def kernel(
     tiles, est, frames, shifts, blur, out,
-    taps_in, xw, yb, fb, fs, sy, sx, xs, px, pg, xb, aa, af, hh, d1, r1, d2, r2, pr,
-    load_sem, ysend, yrecv, hsend, hrecv, fsend, frecv, usend, urecv, ssend, srecv,
+    taps_in, xw, fr, zs, fb, sb, xs, px, pg, xb, aa, af, hh, d1, r1, d2, r2, pr, mine,
+    load_sem, hsend, hrecv, fsend, frecv, ssend, srecv,
     e1send, e1recv, e2send, e2recv, gsend, grecv,
 ):
     t = lax.axis_index("tile")
@@ -60,7 +60,7 @@
     x = f // SIDE
     y = f % SIDE
     c = SIDE * y + x
-    last = SIDE * SIDE - 1
+    last = FRAMES - 1
     at_low = (last - c) // last
     at_high = c // last
     start = pl.multiple_of(128 * (2 * c - 1 + at_low - at_high), 128)
@@ -97,16 +97,16 @@
 
         return Pair()
 
-    def span(target):
-        edge = (SIDE - 1 - target) // (SIDE - 1) - target // (SIDE - 1)
-        source = pl.multiple_of(128 * (SIDE * target - 1 + edge), 128)
-        return frames.at[0, :, pl.ds(source, SPAN)], pl.ds(pl.multiple_of(128 * (1 + edge), 128), SPAN)
+    def peer(slot):
+        px_, py_ = lax.rem(x + slot // SIDE, SIDE), lax.rem(y + slot % SIDE, SIDE)
+        return {"frame": SIDE * px_ + py_}, SIDE * py_ + px_
+
+    order = sorted(range(1, FRAMES), key=lambda slot: -(min(slot // SIDE, 4 - slot // SIDE) + 2 * min(slot % SIDE, 4 - slot % SIDE)))
 
     window = est.at[:, pl.ds(start, 512)]
-    own_span, own_lanes = span(y)
-    load_f = pltpu.make_async_copy(own_span, yb.at[0, :, own_lanes], load_sem.at[0])
+    load_f = pltpu.make_async_copy(frames.at[0], fr, load_sem.at[0])
     load_x = pltpu.make_async_copy(window, xw.at[pl.ds(ROWS, ROWS), pl.ds(lane0, 512)], load_sem.at[1])
-    load_s = pltpu.make_async_copy(shifts, sy.at[0], load_sem.at[2])
+    load_s = pltpu.make_async_copy(shifts, sb.at[0], load_sem.at[2])
     load_b = pltpu.make_async_copy(blur, taps_in, load_sem.at[3])
 
     barrier = pltpu.get_barrier_semaphore()
@@ -114,17 +114,23 @@
     def greet(device):
         pl.semaphore_signal(barrier, inc=1, device_id=device, device_id_type=MESH)
 
-    for e in (2, 1, 3):
-        greet(ypeer(e))
-    for e in (2, 1, 3):
-        greet(xpeer(e))
+    load_f.start()
+    for slot in order:
+        greet(peer(slot)[0])
     pl.when(t > 0)(lambda: greet({"tile": up}))
     pl.when(t < tiles - 1)(lambda: greet({"tile": down}))
-    load_f.start()
     load_x.start()
     load_s.start()
     load_b.start()
-    pl.semaphore_wait(barrier, 2 * SIDE - 1 + (t + tiles - 1) // tiles - (t + 1) // tiles)
+
+    load_f.wait()
+    lane = iota((8, 128), 1)
+    before = jnp.zeros((8, 128), F32)
+    for tile in range(FRAMES + 1):
+        rolled = pltpu.roll(fr[:, 128 * tile : 128 * tile + 128], EDGE, 1) if tile < FRAMES else jnp.zeros((8, 128), F32)
+        zs[:, 128 * tile : 128 * tile + 128] = jnp.where(lane < EDGE, before, rolled)
+        before = rolled
+    pl.semaphore_wait(barrier, FRAMES + (t + tiles - 1) // tiles - (t + 1) // tiles)
 
     started = []
 
@@ -133,35 +139,23 @@
         started.append(copy)
         return copy
 
-    ycopies = {}
-    ucopies = {}
-    for e in (2, 1, 3):
-        source, lanes = span(lax.rem(y + e, SIDE))
-        ucopies[e] = go(remote(shifts, sy.at[e], usend.at[e], urecv.at[e], ypeer(e)))
-        ycopies[e] = go(remote(source, yb.at[e, :, lanes], ysend.at[e], yrecv.at[e], ypeer(e)))
+    fcopies = {}
+    scopies = {}
+    for slot in order:
+        scopies[slot] = go(remote(shifts, sb.at[slot], ssend.at[slot], srecv.at[slot], peer(slot)[0]))
     halo = go(
         across_tiles(
             remote(window, xw.at[pl.ds(2 * ROWS, ROWS), pl.ds(lane0, 512)], hsend.at[0], hrecv.at[1], {"tile": up}),
             remote(window, xw.at[pl.ds(0, ROWS), pl.ds(lane0, 512)], hsend.at[1], hrecv.at[0], {"tile": down}),
         )
     )
-    fcopies = {}
-    scopies = {}
-
-    def forward(ey):
-        for ex in (2, 1, 3):
-            target = pl.multiple_of(LOW * lax.rem(x + ex, SIDE) + 128, 128)
-            slot = SIDE * ex + ey
-            scopies[slot] = go(remote(sy.at[ey], sx.at[ex, ey], ssend.at[slot], srecv.at[slot], xpeer(ex)))
-            fcopies[slot] = go(
-                remote(yb.at[ey, :, pl.ds(target, PIECE)], fb.at[ex, ey], fsend.at[slot], frecv.at[slot], xpeer(ex))
-            )
-
-    load_f.wait()
-    load_s.wait()
-    forward(0)
-
-    high_cols = CHUNK * SIDE * SIDE
+    for slot in order:
+        device, chunk = peer(slot)
+        source = zs.at[:, pl.ds(pl.multiple_of(LOW * chunk, LOW), PIECE)]
+        fcopies[slot] = go(remote(source, fb.at[slot], fsend.at[slot], frecv.at[slot], device))
+    fb[0] = zs[:, pl.ds(pl.multiple_of(LOW * c, LOW), PIECE)]
+
+    high_cols = CHUNK * FRAMES
     load_x.wait()
     halo.wait_recv()
     row = ROWS * t - ROWS + iota((3 * ROWS, 512), 0)
@@ -213,22 +207,17 @@
     stage_model(REACH)
     stage_prior(0, 3 * ROWS)
 
-    for ey in (1, 3, 2):
-        ucopies[ey].wait_recv()
-        ycopies[ey].wait_recv()
-        forward(ey)
-
     for phase in range(2):
         pr[phase] = xs[phase, REACH : REACH + BAND] - 0.005 * prior(phase, REACH, BAND)
 
+    load_s.wait()
     for copy in scopies.values():
         copy.wait_recv()
     frame = iota((1, 128), 1) // 8
     down_shift = jnp.zeros((1, 128), jnp.int32)
     side_shift = jnp.zeros((1, 128), jnp.int32)
-    for slot in range(SIDE * SIDE):
-        ex, ey = slot // SIDE, slot % SIDE
-        pair = sx[ex, ey] if ex else sy[ey]
+    for slot in range(FRAMES):
+        pair = sb[slot]
         down_shift = jnp.where(frame == slot, pair[0:1, 0:1], down_shift)
         side_shift = jnp.where(frame == slot, pair[0:1, 1:2], side_shift)
     load_b.wait()
@@ -253,27 +242,21 @@
         af[:, 128 * block : 128 * block + 128] = aa[128 * block : 128 * block + 128].T
 
     low = LOW * c - EDGE + iota((128, 256), 1)
-    live = (low >= 0) & (low < LOW * SIDE * SIDE)
+    live = (low >= 0) & (low < LOW * FRAMES)
 
     def misfits():
         pred = jnp.dot(af[...], xb[...], precision=lax.Precision.HIGH, preferred_element_type=F32)
         return pred
 
     def adjoint(pred):
-        gap = jnp.where(live, jnp.tanh(pred - fs[...]), 0.0)
+        gap = jnp.where(live, jnp.tanh(pred - fb[...].reshape(128, PIECE)), 0.0)
         hh[...] = jnp.dot(
             aa[: OFFS * BAND], gap, precision=lax.Precision.HIGH, preferred_element_type=F32
         )
 
     pred = misfits()
-    for slot in range(SIDE * SIDE):
-        ex, ey = slot // SIDE, slot % SIDE
-        if ex:
-            fcopies[slot].wait_recv()
-            piece = fb[ex, ey]
-        else:
-            piece = yb[ey, :, pl.ds(pl.multiple_of(LOW * x + 128, 128), PIECE)]
-        fs[8 * slot : 8 * slot + 8] = left(piece, 128 - EDGE)[:, :256]
+    for copy in fcopies.values():
+        copy.wait_recv()
     adjoint(pred)
     for phase in range(2):
         total = jnp.zeros((BAND, 256), F32)
@@ -313,8 +296,8 @@
 
     stage_prior(REACH, BAND)
     for phase in range(2):
-        mine = xs[phase, ROWS : 2 * ROWS] - 0.005 * prior(phase, ROWS, ROWS)
-        both[phase] = left(mine, ROWS)[:, :128] - 0.1 * both[phase]
+        kept = xs[phase, ROWS : 2 * ROWS] - 0.005 * prior(phase, ROWS, ROWS)
+        both[phase] = left(kept, ROWS)[:, :128] - 0.1 * both[phase]
     lane_in = iota((CHUNK, CHUNK), 0)
     lane_out = iota((CHUNK, CHUNK), 1)
     table = jnp.where(lane_out == jnp.where(lane_in < LOW, 2 * lane_in, 2 * lane_in - CHUNK + 1), 1.0, 0.0).astype(BF16)
@@ -331,23 +314,27 @@
         source = SIDE * lax.rem(y + SIDE - ey, SIDE) + x
         return out.at[:, pl.ds(pl.multiple_of(CHUNK * source, CHUNK), CHUNK)]
 
-    out[:, pl.ds(pl.multiple_of(CHUNK * c, CHUNK), CHUNK)] = result
+    mine[...] = result
+    keep = pltpu.make_async_copy(mine, chunk_of(0), load_sem.at[4])
     gathers = {}
     for e in (2, 1, 3):
-        gathers[e] = go(remote(chunk_of(0), chunk_of(0), gsend.at[e], grecv.at[e], ypeer(e)))
+        gathers[e] = go(remote(mine, chunk_of(0), gsend.at[e], grecv.at[e], ypeer(e)))
 
     def spread(ey):
+        source = chunk_of(ey) if ey else mine
         for ex in (2, 1, 3):
             slot = SIDE * ex + ey
-            gathers[slot] = go(remote(chunk_of(ey), chunk_of(ey), gsend.at[slot], grecv.at[slot], xpeer(ex)))
+            gathers[slot] = go(remote(source, chunk_of(ey), gsend.at[slot], grecv.at[slot], xpeer(ex)))
 
     spread(0)
+    keep.start()
     for ey in (1, 3, 2):
         gathers[ey].wait_recv()
         spread(ey)
     for slot, copy in gathers.items():
         if slot >= SIDE:
             copy.wait_recv()
+    keep.wait()
     for copy in started:
         copy.wait_send()
 
@@ -355,20 +342,18 @@
 def local(tiles, estimate, frames, shifts, blur):
     vmem = lambda *shape: pltpu.VMEM(shape, F32)
     dma = lambda n: pltpu.SemaphoreType.DMA((n,))
-    both = SIDE * SIDE
     return pl.pallas_call(
         functools.partial(kernel, tiles),
         out_shape=jax.ShapeDtypeStruct(estimate.shape, F32),
-        in_specs=[pl.BlockSpec(memory_space=pl.ANY)] * 4,
-        out_specs=pl.BlockSpec(memory_space=pltpu.VMEM),
+        in_specs=[pl.BlockSpec(memory_space=pltpu.HBM)] * 4,
+        out_specs=pl.BlockSpec(memory_space=pl.ANY),
         scratch_shapes=[
             pltpu.SMEM((TAPS,), F32),
             vmem(3 * ROWS, 768),
-            vmem(SIDE, 8, SPAN + 256),
-            vmem(SIDE, SIDE, 8, PIECE),
-            vmem(128, 256),
-            pltpu.VMEM((SIDE, 1, 2), jnp.int32),
-            pltpu.VMEM((SIDE, SIDE, 1, 2), jnp.int32),
+            vmem(8, FRAMES * LOW),
+            vmem(8, FRAMES * LOW + 128),
+            vmem(FRAMES, 8, PIECE),
+            pltpu.VMEM((FRAMES, 1, 2), jnp.int32),
             vmem(2, 3 * ROWS, 256),
             vmem(6, 3 * ROWS, 256),
             vmem(3, 3 * ROWS, 256),
@@ -381,11 +366,12 @@
             vmem(2, 2, REACH, 128),
             vmem(2, 2, REACH, 128),
             vmem(2, BAND, 256),
-            dma(4), dma(SIDE), dma(SIDE), dma(2), dma(2), dma(both), dma(both), dma(SIDE), dma(SIDE), dma(both), dma(both),
-            dma(2), dma(2), dma(2), dma(2), dma(both), dma(both),
+            vmem(ROWS, CHUNK),
+            dma(5), dma(2), dma(2), dma(FRAMES), dma(FRAMES), dma(FRAMES), dma(FRAMES),
+            dma(2), dma(2), dma(2), dma(2), dma(FRAMES), dma(FRAMES),
         ],
-        compiler_params=pltpu.CompilerParams(collective_id=0, has_side_effects=True),
-    )(estimate, frames, shifts, blur)
+        compiler_params=pltpu.CompilerParams(collective_id=0, has_side_effects=True, vmem_limit_bytes=16 * 1024 * 1024),
+    )(*(pltpu.with_memory_space_constraint(value, pltpu.HBM) for value in (estimate, frames, shifts, blur)))
 
 
 def solution(mesh):

time: 38.6 us -> 35.6 us (0.922)
  Pallas kernels: 36.7 us -> 34.7 us
  local copies, waits for them, and re-layouts: 1.67 us -> 0.71 us
    pallas_call x1, Pallas kernels: 36.7 us -> 34.7 us  [local(): pl.pallas_call(functools.partial(kernel, tiles), out_shape=jax.ShapeDtype...]
    unnamed x1, local copies, waits for them, and re-layouts: 1.67 us -> 0.71 us
where the time goes in v3:
time: 35.6 us; the launch traced here: 35.4 us
  Pallas kernels  34.7 us (97%)
  local copies, waits for them, and re-layouts  0.71 us (2%)
    pallas_call x1, Pallas kernels, local(): pl.pallas_call(functools.partial(kernel, tiles), out_shape=jax.ShapeDtype...  34.7 us

profile of v3, /device:TPU:256, one launch (start us, length us, event | category | flops | bytes accessed | tf_op | source)
XLA Modules:
  0.0 35.4 jit_solution(949565073056024718)
XLA Ops:
  0.0 34.7 %shard_map.46 = f32[16,4096]{1,0:T(8,128)S(1)} custom-call(f32[16,4096]{1,0:T(8,128)} %est.1, f32[1,8,2048]{2,1,0:T(8,128)} %frames.1, s32[1,2]{1,0:T(1,128)} %shifts.1, f32[7]{0:T(128)} %blur.1), custom_call_target="tpu_custom_call" | custom-call | tf_op jit(solution)/shard_map/pallas_call | solution.py:345
  34.7 0.7 %copy.6 = f32[16,4096]{1,0:T(8,128)} copy(f32[16,4096]{1,0:T(8,128)S(1)} %shard_map.46) | data formatting | bytes 524288

commit v4 on v3

--- a/solution.py
+++ b/solution.py
@@ -68,12 +68,6 @@
     up = lax.rem(t + tiles - 1, tiles)
     down = lax.rem(t + 1, tiles)
 
-    def ypeer(e):
-        return {"frame": SIDE * x + lax.rem(y + e, SIDE)}
-
-    def xpeer(e):
-        return {"frame": SIDE * lax.rem(x + e, SIDE) + y}
-
     def remote(src, dst, send, recv, device):
         return pltpu.make_async_remote_copy(
             src_ref=src, dst_ref=dst, send_sem=send, recv_sem=recv, device_id=device, device_id_type=MESH
@@ -310,30 +304,13 @@
         halves.append(both[phase] - 0.1 * jnp.where(edge_row, 0.0, theirs))
     result = pick(jnp.concatenate(halves, axis=1), table)
 
-    def chunk_of(ey):
-        source = SIDE * lax.rem(y + SIDE - ey, SIDE) + x
-        return out.at[:, pl.ds(pl.multiple_of(CHUNK * source, CHUNK), CHUNK)]
-
     mine[...] = result
-    keep = pltpu.make_async_copy(mine, chunk_of(0), load_sem.at[4])
-    gathers = {}
-    for e in (2, 1, 3):
-        gathers[e] = go(remote(mine, chunk_of(0), gsend.at[e], grecv.at[e], ypeer(e)))
-
-    def spread(ey):
-        source = chunk_of(ey) if ey else mine
-        for ex in (2, 1, 3):
-            slot = SIDE * ex + ey
-            gathers[slot] = go(remote(source, chunk_of(ey), gsend.at[slot], grecv.at[slot], xpeer(ex)))
-
-    spread(0)
+    own = out.at[:, pl.ds(pl.multiple_of(CHUNK * c, CHUNK), CHUNK)]
+    keep = pltpu.make_async_copy(mine, own, load_sem.at[4])
+    gathers = {slot: go(remote(mine, own, gsend.at[slot], grecv.at[slot], peer(slot)[0])) for slot in order}
     keep.start()
-    for ey in (1, 3, 2):
-        gathers[ey].wait_recv()
-        spread(ey)
-    for slot, copy in gathers.items():
-        if slot >= SIDE:
-            copy.wait_recv()
+    for copy in gathers.values():
+        copy.wait_recv()
     keep.wait()
     for copy in started:
         copy.wait_send()

time: 35.6 us -> 34 us (0.955)
  Pallas kernels: 34.7 us -> 33.1 us
    pallas_call x1, Pallas kernels: 34.7 us -> 33.1 us  [local(): pl.pallas_call(functools.partial(kernel, tiles), out_shape=jax.ShapeDtype...]
where the time goes in v4:
time: 34 us; the launch traced here: 33.8 us
  Pallas kernels  33.1 us (97%)
  local copies, waits for them, and re-layouts  0.71 us (2%)
    pallas_call x1, Pallas kernels, local(): pl.pallas_call(functools.partial(kernel, tiles), out_shape=jax.ShapeDtype...  33.1 us
    unnamed x1, local copies, waits for them, and re-layouts  0.71 us

profile of v4, /device:TPU:256, one launch (start us, length us, event | category | flops | bytes accessed | tf_op | source)
XLA Modules:
  0.0 33.8 jit_solution(11809929372779494891)
XLA Ops:
  0.0 33.1 %shard_map.46 = f32[16,4096]{1,0:T(8,128)S(1)} custom-call(f32[16,4096]{1,0:T(8,128)} %est.1, f32[1,8,2048]{2,1,0:T(8,128)} %frames.1, s32[1,2]{1,0:T(1,128)} %shifts.1, f32[7]{0:T(128)} %blur.1), custom_call_target="tpu_custom_call" | custom-call | tf_op jit(solution)/shard_map/pallas_call | solution.py:322
  33.1 0.7 %copy.6 = f32[16,4096]{1,0:T(8,128)} copy(f32[16,4096]{1,0:T(8,128)S(1)} %shard_map.46) | data formatting | bytes 524288

commit v5 on v4

--- a/solution.py
+++ b/solution.py
@@ -18,7 +18,7 @@
 EDGE = 12
 ROWS = 16
 BAND = 2 * ROWS
-PIECE = 256
+SLOT = 32
 FRAMES = SIDE * SIDE
 KDIM = 640
 MESH = pl.DeviceIdType.MESH
@@ -51,7 +51,7 @@
 
 def kernel(
     tiles, est, frames, shifts, blur, out,
-    taps_in, xw, fr, zs, fb, sb, xs, px, pg, xb, aa, af, hh, d1, r1, d2, r2, pr, mine,
+    taps_in, shift_in, xw, fr, zs, zp, fb, hp, fh, xs, px, pg, xh, xl, aa, a3, af, hh, d1, r1, d2, r2, pr, mine,
     load_sem, hsend, hrecv, fsend, frecv, ssend, srecv,
     e1send, e1recv, e2send, e2recv, gsend, grecv,
 ):
@@ -100,7 +100,7 @@
     window = est.at[:, pl.ds(start, 512)]
     load_f = pltpu.make_async_copy(frames.at[0], fr, load_sem.at[0])
     load_x = pltpu.make_async_copy(window, xw.at[pl.ds(ROWS, ROWS), pl.ds(lane0, 512)], load_sem.at[1])
-    load_s = pltpu.make_async_copy(shifts, sb.at[0], load_sem.at[2])
+    load_s = pltpu.make_async_copy(shifts, shift_in, load_sem.at[2])
     load_b = pltpu.make_async_copy(blur, taps_in, load_sem.at[3])
 
     barrier = pltpu.get_barrier_semaphore()
@@ -109,21 +109,33 @@
         pl.semaphore_signal(barrier, inc=1, device_id=device, device_id_type=MESH)
 
     load_f.start()
+    load_s.start()
     for slot in order:
         greet(peer(slot)[0])
     pl.when(t > 0)(lambda: greet({"tile": up}))
     pl.when(t < tiles - 1)(lambda: greet({"tile": down}))
     load_x.start()
-    load_s.start()
     load_b.start()
 
     load_f.wait()
     lane = iota((8, 128), 1)
+    sub = iota((8, 128), 0)
     before = jnp.zeros((8, 128), F32)
+    load_s.wait()
+    tail = jnp.where(
+        lane == 2 * EDGE, jnp.full((8, 128), shift_in[0, 0].astype(F32)), jnp.full((8, 128), shift_in[0, 1].astype(F32))
+    )
     for tile in range(FRAMES + 1):
         rolled = pltpu.roll(fr[:, 128 * tile : 128 * tile + 128], EDGE, 1) if tile < FRAMES else jnp.zeros((8, 128), F32)
         zs[:, 128 * tile : 128 * tile + 128] = jnp.where(lane < EDGE, before, rolled)
         before = rolled
+        if tile:
+            part = jnp.where(lane < 2 * EDGE, zs[:, 128 * tile : 128 * tile + 128], tail)
+            part = jnp.where(lane < SLOT, part, 0.0)
+            for turn in range(1, 4):
+                part = jnp.where(sub % 4 == turn, pltpu.roll(part, 128 - SLOT * turn, 1), part)
+            zp[tile - 1, 0:1] = jnp.sum(jnp.where(sub < 4, part, 0.0), axis=0, keepdims=True)
+            zp[tile - 1, 1:2] = jnp.sum(jnp.where(sub < 4, 0.0, part), axis=0, keepdims=True)
     pl.semaphore_wait(barrier, FRAMES + (t + tiles - 1) // tiles - (t + 1) // tiles)
 
     started = []
@@ -136,7 +148,8 @@
     fcopies = {}
     scopies = {}
     for slot in order:
-        scopies[slot] = go(remote(shifts, sb.at[slot], ssend.at[slot], srecv.at[slot], peer(slot)[0]))
+        device, chunk = peer(slot)
+        scopies[slot] = go(remote(zp.at[chunk], hp.at[slot], ssend.at[slot], srecv.at[slot], device))
     halo = go(
         across_tiles(
             remote(window, xw.at[pl.ds(2 * ROWS, ROWS), pl.ds(lane0, 512)], hsend.at[0], hrecv.at[1], {"tile": up}),
@@ -145,9 +158,10 @@
     )
     for slot in order:
         device, chunk = peer(slot)
-        source = zs.at[:, pl.ds(pl.multiple_of(LOW * chunk, LOW), PIECE)]
+        source = zs.at[:, pl.ds(pl.multiple_of(LOW * chunk, LOW), LOW)]
         fcopies[slot] = go(remote(source, fb.at[slot], fsend.at[slot], frecv.at[slot], device))
-    fb[0] = zs[:, pl.ds(pl.multiple_of(LOW * c, LOW), PIECE)]
+    fb[0] = zs[:, pl.ds(pl.multiple_of(LOW * c, LOW), LOW)]
+    hp[0] = zp[c]
 
     high_cols = CHUNK * FRAMES
     load_x.wait()
@@ -170,9 +184,14 @@
     pg[1] = gain
     pg[2] = left(gain, 1)
 
+    def split(value):
+        high = value.astype(BF16)
+        return high, (value - high.astype(F32)).astype(BF16)
+
     def stage_model(lo):
         for off in range(OFFS):
-            xb[BAND * off : BAND * off + BAND] = left(xs[off % 2, lo : lo + BAND], off // 2)
+            rows = slice(BAND * off, BAND * off + BAND)
+            xh[rows], xl[rows] = split(left(xs[off % 2, lo : lo + BAND], off // 2))
 
     def stage_prior(lo, count):
         for phase in range(2):
@@ -196,7 +215,8 @@
                 total = total + (weight * slope) * pg[lanes, rows]
         return total
 
-    xb[OFFS * BAND : KDIM] = jnp.zeros((KDIM - OFFS * BAND, 256), F32)
+    xh[OFFS * BAND : KDIM] = jnp.zeros((KDIM - OFFS * BAND, 256), BF16)
+    xl[OFFS * BAND : KDIM] = jnp.zeros((KDIM - OFFS * BAND, 256), BF16)
     aa[OFFS * BAND : KDIM] = jnp.zeros((KDIM - OFFS * BAND, 128), F32)
     stage_model(REACH)
     stage_prior(0, 3 * ROWS)
@@ -204,16 +224,20 @@
     for phase in range(2):
         pr[phase] = xs[phase, REACH : REACH + BAND] - 0.005 * prior(phase, REACH, BAND)
 
-    load_s.wait()
     for copy in scopies.values():
         copy.wait_recv()
     frame = iota((1, 128), 1) // 8
-    down_shift = jnp.zeros((1, 128), jnp.int32)
-    side_shift = jnp.zeros((1, 128), jnp.int32)
+    down_shift = jnp.zeros((1, 128), F32)
+    side_shift = jnp.zeros((1, 128), F32)
     for slot in range(FRAMES):
-        pair = sb[slot]
-        down_shift = jnp.where(frame == slot, pair[0:1, 0:1], down_shift)
-        side_shift = jnp.where(frame == slot, pair[0:1, 1:2], side_shift)
+        down_shift = jnp.where(frame == slot, hp[slot, 0:1, 2 * EDGE : 2 * EDGE + 1], down_shift)
+        side_shift = jnp.where(frame == slot, hp[slot, 0:1, 2 * EDGE + 1 : 2 * EDGE + 2], side_shift)
+        rows = jnp.where(
+            sub < 4, jnp.broadcast_to(hp[slot, 0:1], (8, 128)), jnp.broadcast_to(hp[slot, 1:2], (8, 128))
+        )
+        for _ in range(2):
+            rows = pltpu.roll(rows, 0, 1, stride=SLOT // 2, stride_axis=0)
+        fh[8 * slot : 8 * slot + 8] = rows
     load_b.wait()
     blur_sum = taps_in[0]
     for tap in range(1, TAPS):
@@ -224,29 +248,33 @@
     def tap_at(distance):
         total = jnp.zeros(distance.shape, F32)
         for tap in range(TAPS):
-            total = jnp.where(distance == tap - RADIUS, jnp.broadcast_to(taps[tap], distance.shape), total)
+            total = jnp.where(distance == float(tap - RADIUS), jnp.broadcast_to(taps[tap], distance.shape), total)
         return total
 
-    place = iota((BAND, 128), 0) - REACH - 2 * (iota((BAND, 128), 1) % 8)
+    place = (iota((BAND, 128), 0) - REACH - 2 * (iota((BAND, 128), 1) % 8)).astype(F32)
     by_row = tap_at(place - down_shift)
-    by_col = tap_at(iota((24, 128), 0) - REACH - side_shift)
+    by_col = tap_at((iota((24, 128), 0) - REACH).astype(F32) - side_shift)
     for off in range(OFFS):
-        aa[BAND * off : BAND * off + BAND] = by_row * by_col[off : off + 1]
+        rows = slice(BAND * off, BAND * off + BAND)
+        entry = by_row * by_col[off : off + 1]
+        aa[rows] = entry
+        a3[rows, 0:128], a3[rows, 128:256] = split(entry)
+        a3[rows, 256:384] = a3[rows, 0:128]
     for block in range(KDIM // 128):
-        af[:, 128 * block : 128 * block + 128] = aa[128 * block : 128 * block + 128].T
+        columns = slice(128 * block, 128 * block + 128)
+        af[:128, columns], af[128:, columns] = split(aa[128 * block : 128 * block + 128].T)
 
     low = LOW * c - EDGE + iota((128, 256), 1)
     live = (low >= 0) & (low < LOW * FRAMES)
 
     def misfits():
-        pred = jnp.dot(af[...], xb[...], precision=lax.Precision.HIGH, preferred_element_type=F32)
-        return pred
+        both = jnp.dot(af[...], xh[...], preferred_element_type=F32)
+        return both[:128] + both[128:] + jnp.dot(af[:128], xl[...], preferred_element_type=F32)
 
     def adjoint(pred):
-        gap = jnp.where(live, jnp.tanh(pred - fb[...].reshape(128, PIECE)), 0.0)
-        hh[...] = jnp.dot(
-            aa[: OFFS * BAND], gap, precision=lax.Precision.HIGH, preferred_element_type=F32
-        )
+        seen = jnp.concatenate([fb[...].reshape(128, LOW), fh[...]], axis=1)
+        high, rest = split(jnp.where(live, jnp.tanh(pred - seen), 0.0))
+        hh[...] = jnp.dot(a3[...], jnp.concatenate([high, high, rest], axis=0), preferred_element_type=F32)
 
     pred = misfits()
     for copy in fcopies.values():
@@ -326,17 +354,22 @@
         out_specs=pl.BlockSpec(memory_space=pl.ANY),
         scratch_shapes=[
             pltpu.SMEM((TAPS,), F32),
+            pltpu.SMEM((1, 2), jnp.int32),
             vmem(3 * ROWS, 768),
             vmem(8, FRAMES * LOW),
             vmem(8, FRAMES * LOW + 128),
-            vmem(FRAMES, 8, PIECE),
-            pltpu.VMEM((FRAMES, 1, 2), jnp.int32),
+            vmem(FRAMES, 2, 128),
+            vmem(FRAMES, 8, LOW),
+            vmem(FRAMES, 2, 128),
+            vmem(128, 128),
             vmem(2, 3 * ROWS, 256),
             vmem(6, 3 * ROWS, 256),
             vmem(3, 3 * ROWS, 256),
-            vmem(KDIM, 256),
+            pltpu.VMEM((KDIM, 256), BF16),
+            pltpu.VMEM((KDIM, 256), BF16),
             vmem(KDIM, 128),
-            vmem(128, KDIM),
+            pltpu.VMEM((OFFS * BAND, 384), BF16),
+            pltpu.VMEM((256, KDIM), BF16),
             vmem(OFFS * BAND, 256),
             vmem(2, BAND, 256),
             vmem(2, BAND, 256),

time: 34 us -> 32.9 us (0.968)
  Pallas kernels: 33.1 us -> 32.1 us
    pallas_call x1, Pallas kernels: 33.1 us -> 32.1 us  [local(): pl.pallas_call(functools.partial(kernel, tiles), out_shape=jax.ShapeDtype...]
where the time goes in v5:
time: 32.9 us; the launch traced here: 32.8 us
  Pallas kernels  32.1 us (98%)
  local copies, waits for them, and re-layouts  0.71 us (2%)
    pallas_call x1, Pallas kernels, local(): pl.pallas_call(functools.partial(kernel, tiles), out_shape=jax.ShapeDtype...  32.1 us
    unnamed x1, local copies, waits for them, and re-layouts  0.71 us

profile of v5, /device:TPU:256, one launch (start us, length us, event | category | flops | bytes accessed | tf_op | source)
XLA Modules:
  0.0 32.8 jit_solution(13982509916815504514)
XLA Ops:
  0.0 32.1 %shard_map.46 = f32[16,4096]{1,0:T(8,128)S(1)} custom-call(f32[16,4096]{1,0:T(8,128)} %est.1, f32[1,8,2048]{2,1,0:T(8,128)} %frames.1, s32[1,2]{1,0:T(1,128)} %shifts.1, f32[7]{0:T(128)} %blur.1), custom_call_target="tpu_custom_call" | custom-call | tf_op jit(solution)/shard_map/pallas_call | solution.py:350
  32.1 0.7 %copy.6 = f32[16,4096]{1,0:T(8,128)} copy(f32[16,4096]{1,0:T(8,128)S(1)} %shard_map.46) | data formatting | bytes 524288

commit v6 on v5

--- a/solution.py
+++ b/solution.py
@@ -150,16 +150,16 @@
     for slot in order:
         device, chunk = peer(slot)
         scopies[slot] = go(remote(zp.at[chunk], hp.at[slot], ssend.at[slot], srecv.at[slot], device))
+    for slot in order:
+        device, chunk = peer(slot)
+        source = zs.at[:, pl.ds(pl.multiple_of(LOW * chunk, LOW), LOW)]
+        fcopies[slot] = go(remote(source, fb.at[slot], fsend.at[slot], frecv.at[slot], device))
     halo = go(
         across_tiles(
             remote(window, xw.at[pl.ds(2 * ROWS, ROWS), pl.ds(lane0, 512)], hsend.at[0], hrecv.at[1], {"tile": up}),
             remote(window, xw.at[pl.ds(0, ROWS), pl.ds(lane0, 512)], hsend.at[1], hrecv.at[0], {"tile": down}),
         )
     )
-    for slot in order:
-        device, chunk = peer(slot)
-        source = zs.at[:, pl.ds(pl.multiple_of(LOW * chunk, LOW), LOW)]
-        fcopies[slot] = go(remote(source, fb.at[slot], fsend.at[slot], frecv.at[slot], device))
     fb[0] = zs[:, pl.ds(pl.multiple_of(LOW * c, LOW), LOW)]
     hp[0] = zp[c]
 
@@ -219,10 +219,6 @@
     xl[OFFS * BAND : KDIM] = jnp.zeros((KDIM - OFFS * BAND, 256), BF16)
     aa[OFFS * BAND : KDIM] = jnp.zeros((KDIM - OFFS * BAND, 128), F32)
     stage_model(REACH)
-    stage_prior(0, 3 * ROWS)
-
-    for phase in range(2):
-        pr[phase] = xs[phase, REACH : REACH + BAND] - 0.005 * prior(phase, REACH, BAND)
 
     for copy in scopies.values():
         copy.wait_recv()
@@ -294,6 +290,9 @@
     reach_row = ROWS * t - REACH + iota((BAND, 256), 0)
     edge_row = (reach_row < REACH) | (reach_row >= ROWS * tiles - REACH)
     within = pg[1, REACH : REACH + BAND] > 1.5
+    stage_prior(0, 3 * ROWS)
+    for phase in range(2):
+        pr[phase] = xs[phase, REACH : REACH + BAND] - 0.005 * prior(phase, REACH, BAND)
     first.wait_recv()
     for phase in range(2):
         theirs = jnp.where(edge_row, 0.0, r1[phase])
@@ -335,10 +334,41 @@
     mine[...] = result
     own = out.at[:, pl.ds(pl.multiple_of(CHUNK * c, CHUNK), CHUNK)]
     keep = pltpu.make_async_copy(mine, own, load_sem.at[4])
-    gathers = {slot: go(remote(mine, own, gsend.at[slot], grecv.at[slot], peer(slot)[0])) for slot in order}
-    keep.start()
-    for copy in gathers.values():
-        copy.wait_recv()
+    def gather(slot, source, target, device):
+        return remote(source, target, gsend.at[slot], grecv.at[slot], device)
+
+    direct = [gather(slot, mine, own, peer(slot)[0]) for slot in order]
+
+    @pl.when(t % 4 != 1)
+    def _():
+        for copy in direct:
+            copy.start()
+        keep.start()
+        for copy in direct:
+            copy.wait_recv()
+        for copy in direct:
+            copy.wait_send()
+
+    @pl.when(t % 4 == 1)
+    def _():
+        copies = {slot: copy for slot, copy in zip(order, direct) if slot < SIDE or slot % SIDE == 0}
+        for slot in (2, 1, 3, 8, 4, 12):
+            copies[slot].start()
+        keep.start()
+        for ey in (1, 3, 2):
+            copies[ey].wait_recv()
+            source = SIDE * lax.rem(y + SIDE - ey, SIDE) + x
+            passing = out.at[:, pl.ds(pl.multiple_of(CHUNK * source, CHUNK), CHUNK)]
+            for ex in (2, 1, 3):
+                slot = SIDE * ex + ey
+                copies[slot] = gather(slot, passing, passing, peer(SIDE * ex)[0])
+                copies[slot].start()
+        for slot, copy in copies.items():
+            if slot >= SIDE:
+                copy.wait_recv()
+        for copy in copies.values():
+            copy.wait_send()
+
     keep.wait()
     for copy in started:
         copy.wait_send()

time: 32.9 us -> 32.6 us (level)
  Pallas kernels: 32.1 us -> 31.7 us
    pallas_call x1, Pallas kernels: 32.1 us -> 31.7 us  [local(): pl.pallas_call(functools.partial(kernel, tiles), out_shape=jax.ShapeDtype...]
where the time goes in v6:
time: 32.6 us; the launch traced here: 32.5 us
  Pallas kernels  31.7 us (97%)
  local copies, waits for them, and re-layouts  0.71 us (2%)
    pallas_call x1, Pallas kernels, local(): pl.pallas_call(functools.partial(kernel, tiles), out_shape=jax.ShapeDtype...  31.7 us
    unnamed x1, local copies, waits for them, and re-layouts  0.71 us

profile of v6, /device:TPU:256, one launch (start us, length us, event | category | flops | bytes accessed | tf_op | source)
XLA Modules:
  0.0 32.5 jit_solution(5916868167695753413)
XLA Ops:
  0.0 31.7 %shard_map.46 = f32[16,4096]{1,0:T(8,128)S(1)} custom-call(f32[16,4096]{1,0:T(8,128)} %est.1, f32[1,8,2048]{2,1,0:T(8,128)} %frames.1, s32[1,2]{1,0:T(1,128)} %shifts.1, f32[7]{0:T(128)} %blur.1), custom_call_target="tpu_custom_call" | custom-call | tf_op jit(solution)/shard_map/pallas_call | solution.py:380
  31.8 0.7 %copy.6 = f32[16,4096]{1,0:T(8,128)} copy(f32[16,4096]{1,0:T(8,128)S(1)} %shard_map.46) | data formatting | bytes 524288

commit v7 on v6

--- a/solution.py
+++ b/solution.py
@@ -21,6 +21,7 @@
 SLOT = 32
 FRAMES = SIDE * SIDE
 KDIM = 640
+OUTER = OFFS * ROWS
 MESH = pl.DeviceIdType.MESH
 F32 = jnp.float32
 BF16 = jnp.bfloat16
@@ -254,8 +255,12 @@
         rows = slice(BAND * off, BAND * off + BAND)
         entry = by_row * by_col[off : off + 1]
         aa[rows] = entry
-        a3[rows, 0:128], a3[rows, 128:256] = split(entry)
-        a3[rows, 256:384] = a3[rows, 0:128]
+        high, rest = split(entry)
+        for begin, height, place_at in ((0, 8, ROWS * off), (8, ROWS, OUTER + ROWS * off), (24, 8, ROWS * off + 8)):
+            into, of = slice(place_at, place_at + height), slice(begin, begin + height)
+            a3[into, 0:128] = high[of]
+            a3[into, 128:256] = rest[of]
+            a3[into, 256:384] = high[of]
     for block in range(KDIM // 128):
         columns = slice(128 * block, 128 * block + 128)
         af[:128, columns], af[128:, columns] = split(aa[128 * block : 128 * block + 128].T)
@@ -270,17 +275,29 @@
     def adjoint(pred):
         seen = jnp.concatenate([fb[...].reshape(128, LOW), fh[...]], axis=1)
         high, rest = split(jnp.where(live, jnp.tanh(pred - seen), 0.0))
-        hh[...] = jnp.dot(a3[...], jnp.concatenate([high, high, rest], axis=0), preferred_element_type=F32)
+        return jnp.concatenate([high, high, rest], axis=0)
+
+    def spread(block, gap, move, width):
+        rows = slice(OUTER * block, OUTER * block + OUTER)
+        hh[rows] = jnp.dot(a3[rows], gap, preferred_element_type=F32)
+        sums = []
+        for phase in range(2):
+            total = jnp.zeros((ROWS, width), F32)
+            for off in range(phase, OFFS, 2):
+                at = OUTER * block + ROWS * off
+                total = total + left(hh[at : at + ROWS], move - off // 2)[:, :width]
+            sums.append(total)
+        return sums
 
     pred = misfits()
     for copy in fcopies.values():
         copy.wait_recv()
-    adjoint(pred)
-    for phase in range(2):
-        total = jnp.zeros((BAND, 256), F32)
-        for off in range(phase, OFFS, 2):
-            total = total + left(hh[BAND * off : BAND * off + BAND], -(off // 2))
-        d1[phase] = total
+    gap = adjoint(pred)
+    outer, inner = spread(0, gap, 0, 256), spread(1, gap, 0, 256)
+    for phase in range(2):
+        d1[phase, :8] = outer[phase][:8]
+        d1[phase, 8:24] = inner[phase]
+        d1[phase, 24:] = outer[phase][8:]
     first = go(
         across_tiles(
             remote(d1.at[:, pl.ds(0, ROWS)], r1.at[:, pl.ds(ROWS, ROWS)], e1send.at[0], e1recv.at[1], {"tile": up}),
@@ -299,15 +316,11 @@
         xs[phase, REACH : REACH + BAND] = jnp.where(within, pr[phase] - 0.1 * (d1[phase] + theirs), 0.0)
 
     stage_model(REACH)
-    adjoint(misfits())
-    both = []
-    for phase in range(2):
-        total = jnp.zeros((BAND, 128), F32)
-        for off in range(phase, OFFS, 2):
-            total = total + left(hh[BAND * off : BAND * off + BAND], ROWS - off // 2)[:, :128]
-        d2[0, phase] = total[:REACH]
-        d2[1, phase] = total[3 * REACH :]
-        both.append(total[REACH : 3 * REACH])
+    gap = adjoint(misfits())
+    outer = spread(0, gap, ROWS, LOW)
+    for phase in range(2):
+        d2[0, phase] = outer[phase][:8]
+        d2[1, phase] = outer[phase][8:]
     second = go(
         across_tiles(
             remote(d2.at[0], r2.at[1], e2send.at[0], e2recv.at[1], {"tile": up}),
@@ -315,6 +328,7 @@
         )
     )
 
+    both = spread(1, gap, ROWS, LOW)
     stage_prior(REACH, BAND)
     for phase in range(2):
         kept = xs[phase, ROWS : 2 * ROWS] - 0.005 * prior(phase, ROWS, ROWS)

time: 32.6 us -> 32.4 us (level)
  no operation moved by 1% of the time
where the time goes in v7:
time: 32.4 us; the launch traced here: 32.2 us
  Pallas kernels  31.5 us (97%)
  local copies, waits for them, and re-layouts  0.71 us (2%)
    pallas_call x1, Pallas kernels, local(): pl.pallas_call(functools.partial(kernel, tiles), out_shape=jax.ShapeDtype...  31.5 us
    unnamed x1, local copies, waits for them, and re-layouts  0.71 us

profile of v7, /device:TPU:256, one launch (start us, length us, event | category | flops | bytes accessed | tf_op | source)
XLA Modules:
  0.0 32.2 jit_solution(8127925711951116602)
XLA Ops:
  0.0 31.5 %shard_map.46 = f32[16,4096]{1,0:T(8,128)S(1)} custom-call(f32[16,4096]{1,0:T(8,128)} %est.1, f32[1,8,2048]{2,1,0:T(8,128)} %frames.1, s32[1,2]{1,0:T(1,128)} %shifts.1, f32[7]{0:T(128)} %blur.1), custom_call_target="tpu_custom_call" | custom-call | tf_op jit(solution)/shard_map/pallas_call | solution.py:394
  31.5 0.7 %copy.6 = f32[16,4096]{1,0:T(8,128)} copy(f32[16,4096]{1,0:T(8,128)S(1)} %shard_map.46) | data formatting | bytes 524288

commit v8 on v7

--- a/solution.py
+++ b/solution.py
@@ -353,7 +353,8 @@
 
     direct = [gather(slot, mine, own, peer(slot)[0]) for slot in order]
 
-    @pl.when(t % 4 != 1)
+    relays = (t % 2 == 1) & (t != tiles // 2 - 1)
+    @pl.when(jnp.logical_not(relays))
     def _():
         for copy in direct:
             copy.start()
@@ -363,7 +364,7 @@
         for copy in direct:
             copy.wait_send()
 
-    @pl.when(t % 4 == 1)
+    @pl.when(relays)
     def _():
         copies = {slot: copy for slot, copy in zip(order, direct) if slot < SIDE or slot % SIDE == 0}
         for slot in (2, 1, 3, 8, 4, 12):

time: 32.4 us -> 32.4 us (level)
  no operation moved by 1% of the time
where the time goes in v8:
time: 32.4 us; the launch traced here: 32.3 us
  Pallas kernels  31.6 us (98%)
  local copies, waits for them, and re-layouts  0.71 us (2%)
    pallas_call x1, Pallas kernels, local(): pl.pallas_call(functools.partial(kernel, tiles), out_shape=jax.ShapeDtype...  31.6 us
    unnamed x1, local copies, waits for them, and re-layouts  0.71 us

profile of v8, /device:TPU:256, one launch (start us, length us, event | category | flops | bytes accessed | tf_op | source)
XLA Modules:
  0.0 32.3 jit_solution(3016283003736302641)
XLA Ops:
  0.0 31.6 %shard_map.46 = f32[16,4096]{1,0:T(8,128)S(1)} custom-call(f32[16,4096]{1,0:T(8,128)} %est.1, f32[1,8,2048]{2,1,0:T(8,128)} %frames.1, s32[1,2]{1,0:T(1,128)} %shifts.1, f32[7]{0:T(128)} %blur.1), custom_call_target="tpu_custom_call" | custom-call | tf_op jit(solution)/shard_map/pallas_call | solution.py:395
  31.6 0.7 %copy.6 = f32[16,4096]{1,0:T(8,128)} copy(f32[16,4096]{1,0:T(8,128)S(1)} %shard_map.46) | data formatting | bytes 524288

commit v9 on v8

--- a/solution.py
+++ b/solution.py
@@ -21,7 +21,8 @@
 SLOT = 32
 FRAMES = SIDE * SIDE
 KDIM = 640
-OUTER = OFFS * ROWS
+GROUP = 8 * (OFFS + 1)
+GROUPS = (1, 0, 3, 2)
 MESH = pl.DeviceIdType.MESH
 F32 = jnp.float32
 BF16 = jnp.bfloat16
@@ -90,7 +91,9 @@
                 pl.when(has_above)(above.wait_send)
                 pl.when(has_below)(below.wait_send)
 
-        return Pair()
+        pair = Pair()
+        pair.above, pair.below = above, below
+        return pair
 
     def peer(slot):
         px_, py_ = lax.rem(x + slot // SIDE, SIDE), lax.rem(y + slot % SIDE, SIDE)
@@ -256,11 +259,14 @@
         entry = by_row * by_col[off : off + 1]
         aa[rows] = entry
         high, rest = split(entry)
-        for begin, height, place_at in ((0, 8, ROWS * off), (8, ROWS, OUTER + ROWS * off), (24, 8, ROWS * off + 8)):
-            into, of = slice(place_at, place_at + height), slice(begin, begin + height)
+        for place_at, group in enumerate(GROUPS):
+            into = slice(GROUP * place_at + 8 * off, GROUP * place_at + 8 * off + 8)
+            of = slice(8 * group, 8 * group + 8)
             a3[into, 0:128] = high[of]
             a3[into, 128:256] = rest[of]
             a3[into, 256:384] = high[of]
+    for place_at in range(4):
+        a3[GROUP * place_at + 8 * OFFS : GROUP * place_at + GROUP] = jnp.zeros((8, 384), BF16)
     for block in range(KDIM // 128):
         columns = slice(128 * block, 128 * block + 128)
         af[:128, columns], af[128:, columns] = split(aa[128 * block : 128 * block + 128].T)
@@ -277,33 +283,34 @@
         high, rest = split(jnp.where(live, jnp.tanh(pred - seen), 0.0))
         return jnp.concatenate([high, high, rest], axis=0)
 
-    def spread(block, gap, move, width):
-        rows = slice(OUTER * block, OUTER * block + OUTER)
+    def spread(first_at, count, gap, move, width):
+        rows = slice(GROUP * first_at, GROUP * (first_at + count))
         hh[rows] = jnp.dot(a3[rows], gap, preferred_element_type=F32)
-        sums = []
-        for phase in range(2):
-            total = jnp.zeros((ROWS, width), F32)
-            for off in range(phase, OFFS, 2):
-                at = OUTER * block + ROWS * off
-                total = total + left(hh[at : at + ROWS], move - off // 2)[:, :width]
-            sums.append(total)
+        sums = {}
+        for place_at in range(first_at, first_at + count):
+            for phase in range(2):
+                total = jnp.zeros((8, width), F32)
+                for off in range(phase, OFFS, 2):
+                    at = GROUP * place_at + 8 * off
+                    total = total + left(hh[at : at + 8], move - off // 2)[:, :width]
+                sums[GROUPS[place_at], phase] = total
         return sums
 
     pred = misfits()
     for copy in fcopies.values():
         copy.wait_recv()
     gap = adjoint(pred)
-    outer, inner = spread(0, gap, 0, 256), spread(1, gap, 0, 256)
-    for phase in range(2):
-        d1[phase, :8] = outer[phase][:8]
-        d1[phase, 8:24] = inner[phase]
-        d1[phase, 24:] = outer[phase][8:]
-    first = go(
-        across_tiles(
-            remote(d1.at[:, pl.ds(0, ROWS)], r1.at[:, pl.ds(ROWS, ROWS)], e1send.at[0], e1recv.at[1], {"tile": up}),
-            remote(d1.at[:, pl.ds(ROWS, ROWS)], r1.at[:, pl.ds(0, ROWS)], e1send.at[1], e1recv.at[0], {"tile": down}),
-        )
+    first = across_tiles(
+        remote(d1.at[:, pl.ds(0, ROWS)], r1.at[:, pl.ds(ROWS, ROWS)], e1send.at[0], e1recv.at[1], {"tile": up}),
+        remote(d1.at[:, pl.ds(ROWS, ROWS)], r1.at[:, pl.ds(0, ROWS)], e1send.at[1], e1recv.at[0], {"tile": down}),
     )
+    for (group, phase), total in spread(0, 2, gap, 0, 256).items():
+        d1[phase, 8 * group : 8 * group + 8] = total
+    pl.when(t > 0)(first.above.start)
+    for (group, phase), total in spread(2, 2, gap, 0, 256).items():
+        d1[phase, 8 * group : 8 * group + 8] = total
+    pl.when(t < tiles - 1)(first.below.start)
+    started.append(first)
     reach_row = ROWS * t - REACH + iota((BAND, 256), 0)
     edge_row = (reach_row < REACH) | (reach_row >= ROWS * tiles - REACH)
     within = pg[1, REACH : REACH + BAND] > 1.5
@@ -317,10 +324,8 @@
 
     stage_model(REACH)
     gap = adjoint(misfits())
-    outer = spread(0, gap, ROWS, LOW)
-    for phase in range(2):
-        d2[0, phase] = outer[phase][:8]
-        d2[1, phase] = outer[phase][8:]
+    for (group, phase), total in spread(1, 2, gap, ROWS, LOW).items():
+        d2[group // 3, phase] = total
     second = go(
         across_tiles(
             remote(d2.at[0], r2.at[1], e2send.at[0], e2recv.at[1], {"tile": up}),
@@ -328,7 +333,8 @@
         )
     )
 
-    both = spread(1, gap, ROWS, LOW)
+    inner = spread(0, 1, gap, ROWS, LOW) | spread(3, 1, gap, ROWS, LOW)
+    both = [jnp.concatenate([inner[1, phase], inner[2, phase]], axis=0) for phase in range(2)]
     stage_prior(REACH, BAND)
     for phase in range(2):
         kept = xs[phase, ROWS : 2 * ROWS] - 0.005 * prior(phase, ROWS, ROWS)
@@ -413,9 +419,9 @@
             pltpu.VMEM((KDIM, 256), BF16),
             pltpu.VMEM((KDIM, 256), BF16),
             vmem(KDIM, 128),
-            pltpu.VMEM((OFFS * BAND, 384), BF16),
+            pltpu.VMEM((4 * GROUP, 384), BF16),
             pltpu.VMEM((256, KDIM), BF16),
-            vmem(OFFS * BAND, 256),
+            vmem(4 * GROUP, 256),
             vmem(2, BAND, 256),
             vmem(2, BAND, 256),
             vmem(2, 2, REACH, 128),

time: 32.4 us -> 32.3 us (level)
  no operation moved by 1% of the time
where the time goes in v9:
time: 32.3 us; the launch traced here: 32.2 us
  Pallas kernels  31.4 us (97%)
  local copies, waits for them, and re-layouts  0.71 us (2%)
    pallas_call x1, Pallas kernels, local(): pl.pallas_call(functools.partial(kernel, tiles), out_shape=jax.ShapeDtype...  31.4 us
    unnamed x1, local copies, waits for them, and re-layouts  0.71 us

profile of v9, /device:TPU:256, one launch (start us, length us, event | category | flops | bytes accessed | tf_op | source)
XLA Modules:
  0.0 32.2 jit_solution(16925879076952818986)
XLA Ops:
  0.0 31.4 %shard_map.46 = f32[16,4096]{1,0:T(8,128)S(1)} custom-call(f32[16,4096]{1,0:T(8,128)} %est.1, f32[1,8,2048]{2,1,0:T(8,128)} %frames.1, s32[1,2]{1,0:T(1,128)} %shifts.1, f32[7]{0:T(128)} %blur.1), custom_call_target="tpu_custom_call" | custom-call | tf_op jit(solution)/shard_map/pallas_call | solution.py:401
  31.5 0.7 %copy.6 = f32[16,4096]{1,0:T(8,128)} copy(f32[16,4096]{1,0:T(8,128)S(1)} %shard_map.46) | data formatting | bytes 524288
